TPU v7x, 256 devices: a whole 4x4x8 slice. The times are simulated.
256 devices in a mesh: pair: 16 (over y, z_lo, core), virt: 16 (over x, z_hi).
Axes of the slice: x: 4, y: 4, z: 8 (z_hi: 4, z_lo: 2; z = z_hi * 2 + z_lo), core: 2. Of those that a mesh axis runs over, the one named last changes fastest.
Arguments:
- amplitudes: float32 [16384, 1024], P('pair', 'virt'), may hold values from -6 to 6
- integrals: float32 [16384, 1024], P('virt', 'pair'), may hold values from -0.54 to 0.54
- residual_in: float32 [16384, 16384], P('pair', 'virt'), may hold values from -6 to 6
- pair_irrep: int32 [16384], P('pair'), may hold values from 0 to 7
- ab_irrep: int32 [16384], P('virt'), may hold values from 0 to 7
- cd_irrep: int32 [1024], replicated, may hold values from 0 to 7, as said below
Outputs:
- residual: float32 [16384, 16384], P('pair', 'virt')
Inputs may be any that keep to these rules, and one draw needn't show every extreme that they name: `pair_irrep`: irrep labels. `ab_irrep`: irrep labels. `cd_irrep`: in every aligned block of 8 consecutive cd of the window, each of the 8 irreps labels exactly one cd.
All inputs are finite; a program needn't handle non-finite values.
Results may differ from a plain program's by a relative error of at most 0.00005.
Values sent between devices are 32-bit elements; how exact they have to be, the bound alone decides.
No kernel may reach another device: no remote copies, remote signals or barrier semaphores. Data moves between devices by JAX's collectives and lax.ppermute only.
A program may use at most 64 MiB of HBM per device.

v0:
```python
import jax
import jax.numpy as jnp
from jax import lax
from jax.sharding import PartitionSpec as P


def contract(left, right):
    return lax.dot_general(
        left,
        right,
        (((1,), (1,)), ((), ())),
        precision=lax.Precision.HIGHEST,
        preferred_element_type=jnp.float32,
    )


def shards(amplitudes, integrals, residual_in, pair_irrep, ab_irrep, cd_irrep):
    full_t = lax.all_gather(amplitudes, "virt", axis=1, tiled=True)
    masked_t = jnp.where(pair_irrep[:, None] == cd_irrep[None, :], full_t, jnp.float32(0.0))
    masked_v = jnp.where(
        ab_irrep[:, None] == cd_irrep[None, :],
        lax.all_gather(integrals, "pair", axis=1, tiled=True),
        jnp.float32(0.0),
    )
    return residual_in + contract(masked_t, masked_v)


def solution(mesh):
    placed = (P("pair", "virt"), P("virt", "pair"), P("pair", "virt"), P("pair"), P("virt"), P())
    return jax.shard_map(
        shards, mesh=mesh, in_specs=placed, out_specs=P("pair", "virt"), check_vma=False
    )
```

profile of v0, /device:TPU:6, one launch (start us, length us, event | category | flops | bytes accessed | tf_op | source)
XLA Modules:
  0.0 157.5 jit_solution(8752811544899633555)
XLA Ops:
  6.5 0.0 all-gather.3.cloned.1.call-start
  6.5 0.7 all-gather.3.cloned.1.call-update
  7.3 0.0 all-gather.5.cloned.1.call-start
  7.3 0.7 all-gather.5.cloned.1.call-update
  8.0 80.7 %all-gather.3.cloned.1.call-done = f32[1024,1024]{0,1:T(8,128)} async-done(((f32[1024,64]{0,1:T(8,128)}), f32[1024,1024]{0,1:T(8,128)}) %all-gather.3.cloned.1.call-update) | async-done | bytes 4194320 | tf_op jit(solution)/shard_map/all_gather | solution.py:18
  88.7 41.6 %all-gather.5.cloned.1.call-done = f32[1024,1024]{0,1:T(8,128)} async-done(((f32[1024,64]{0,1:T(8,128)}), f32[1024,1024]{0,1:T(8,128)}) %all-gather.5.cloned.1.call-update) | async-done | bytes 4194320 | tf_op jit(solution)/shard_map/all_gather | solution.py:22
  130.3 20.4 %fusion.9 = f32[1024,1024]{1,0:T(8,128)} fusion(f32[1024,1024]{1,0:T(8,128)} %param.8, f32[1024,1024]{0,1:T(8,128)} %all-gather.5.cloned.1.call-done, s32[1024]{0:T(1024)} %param.10, s32[1024]{0:T(1024)} %param.11, f32[1024,1024]{0,1:T(8,128)} %all-gather.3.cloned.1.call-done, s32[1024]{0:T(1024)} %param.9), kind=kOutput, calls=%fused_computation.9 | convolution fusion | flops 12890144768 | bytes 16789504 | tf_op jit(solution)/shard_map/dot_general | solution.py:8
Async XLA Ops:
  6.5 82.1 %all-gather.3.cloned.1.call-start = ((), (), s32[]{:S(2)}) async-start(), calls=%async_computation | async-start | bytes 4456448 | tf_op jit(solution)/shard_map/all_gather | solution.py:18
  7.3 123.1 %all-gather.5.cloned.1.call-start = ((), (), s32[]{:S(2)}) async-start(), calls=%async_computation.1 | async-start | bytes 4456448 | tf_op jit(solution)/shard_map/all_gather | solution.py:22
Sparse Core Ops, SparseCore 0:
  9.8 78.8 all-gather.2
  90.5 39.7 all-gather.4
where the time goes:
time: 159 us; the launch traced here: 158 us
  waiting for transfers between devices  124 us (78%)
  matrix products  20.4 us (13%)
  between operations  13.4 us (8%)
    all_gather x1, waiting for transfers between devices, shards(): full_t = lax.all_gather(amplitudes, 'virt', axis=1, tiled=True)  80.7 us
    all_gather x1, waiting for transfers between devices, shards(): lax.all_gather(integrals, 'pair', axis=1, tiled=True)  41.6 us
    dot_general x1, matrix products, contract(): lax.dot_general(left, right, (((1,), (1,)), ((), ())), precision=lax.Prec...  20.4 us
  transfers between devices with their start and end apart: 2, of which 2 were waited for; matrix products, arithmetic and copies ran while one was open for 0% of the time, Pallas kernels for 0%

commit v1 on v0

v1 whole, which is shorter than its diff:
```python
import jax
import jax.numpy as jnp
from jax import lax
from jax.experimental import pallas as pl
from jax.experimental.pallas import tpu as pltpu
from jax.sharding import PartitionSpec as P

BLOCK = 8
LANES = 128


def column(row):
    return jnp.transpose(jnp.broadcast_to(row, (LANES, LANES)))


def compact_kernel(t_ref, v_ref, pair_ref, ab_ref, cd_ref, ct_ref, cv_ref):
    def one(x_ref, irrep_ref, index, out_ref):
        held = x_ref.shape[0]
        per_row = LANES // held
        labels = column(cd_ref[pl.ds(index // per_row, 1), :])
        part = labels[:held]
        for step in range(1, per_row):
            part = jnp.where(index % per_row == step, labels[step * held : (step + 1) * held], part)
        for group in range(x_ref.shape[1] // LANES):
            lanes = slice(group * LANES, (group + 1) * LANES)
            kept = jnp.where(part == irrep_ref[group : group + 1, :], x_ref[:, lanes], 0.0)
            out_ref[:, lanes] = jnp.sum(kept.reshape(held // BLOCK, BLOCK, LANES), axis=1)

    one(t_ref, pair_ref, lax.axis_index("virt"), ct_ref)
    one(v_ref, ab_ref, lax.axis_index("pair"), cv_ref)


def split(x):
    high = x.astype(jnp.bfloat16)
    low = (x - high.astype(jnp.float32)).astype(jnp.bfloat16)
    return high, low


def ladder_kernel(t_order, v_order, *refs):
    t_refs = refs[: len(t_order)]
    v_refs = refs[len(t_order) : len(t_order) + len(v_order)]
    residual_ref, pair_ref, ab_ref, out_ref, t_rows, v_rows, t_split, v_split = refs[len(t_order) + len(v_order) :]
    step = pl.program_id(0)
    depth = t_rows.shape[0]

    @pl.when(step == 0)
    def _():
        apart = lax.axis_index("virt") ^ lax.axis_index("pair")
        for order, ref in zip(t_order, t_refs):
            for slot, k in enumerate(order):
                at = pl.multiple_of((apart ^ k) * BLOCK, BLOCK)
                t_rows[pl.ds(at, BLOCK), :] = ref[slot * BLOCK : (slot + 1) * BLOCK, :]
        for order, ref in zip(v_order, v_refs):
            for slot, k in enumerate(order):
                v_rows[k * BLOCK : (k + 1) * BLOCK, :] = ref[slot * BLOCK : (slot + 1) * BLOCK, :]
        high, low = split(v_rows[...])
        v_split[:depth, :] = high
        v_split[depth : 2 * depth, :] = low
        v_split[2 * depth :, :] = high
        for group in range(t_rows.shape[1] // LANES):
            rows = slice(group * LANES, (group + 1) * LANES)
            high, low = split(jnp.transpose(t_rows[:, rows]))
            t_split[rows, :depth] = high
            t_split[rows, depth : 2 * depth] = high
            t_split[rows, 2 * depth :] = low

    rows = out_ref.shape[0]
    products = jnp.dot(
        t_split[pl.ds(pl.multiple_of(step * rows, rows), rows), :], v_split[...], preferred_element_type=jnp.float32
    )
    labels = column(pair_ref[pl.ds(step, 1), :])
    for group in range(out_ref.shape[1] // LANES):
        lanes = slice(group * LANES, (group + 1) * LANES)
        same = labels == ab_ref[group : group + 1, :]
        out_ref[:, lanes] = residual_ref[:, lanes] + jnp.where(same, products[:, lanes], 0.0)


def pairs(k):
    return [(i, i ^ k) for i in range(16)]


def gather(x, axis, stages):
    held, order = x, [0]
    for stage in stages[:-1]:
        pieces = [held] + [lax.ppermute(held, axis, pairs(k)) for k in stage]
        order = [o ^ k for k in (0, *stage) for o in order]
        held = jnp.concatenate(pieces, 0)
    pieces = [held] + [lax.ppermute(held, axis, pairs(k)) for k in stages[-1]]
    return pieces, [tuple(o ^ k for o in order) for k in (0, *stages[-1])]


def shards(amplitudes, integrals, residual_in, pair_irrep, ab_irrep, cd_irrep):
    rows, columns = residual_in.shape
    held_t, held_v = amplitudes.shape[1], integrals.shape[1]
    pair_rows = pair_irrep.reshape(-1, LANES)
    ab_rows = ab_irrep.reshape(-1, LANES)
    own_t, own_v = pl.pallas_call(
        compact_kernel,
        out_shape=(
            jax.ShapeDtypeStruct((held_t // BLOCK, rows), jnp.float32),
            jax.ShapeDtypeStruct((held_v // BLOCK, columns), jnp.float32),
        ),
        name="compact",
    )(amplitudes.T, integrals.T, pair_rows, ab_rows, cd_irrep.reshape(-1, LANES))
    t_pieces, t_order = gather(own_t, "virt", ((1, 3, 2), (4, 12, 8)))
    v_pieces, v_order = gather(own_v, "pair", ((8, 4, 12), (2,), (1,)))
    depth = 16 * BLOCK
    tile = LANES
    whole = pl.BlockSpec(memory_space=pltpu.VMEM)
    return pl.pallas_call(
        lambda *refs: ladder_kernel(t_order, v_order, *refs),
        grid=(rows // tile,),
        in_specs=[whole] * (len(t_pieces) + len(v_pieces))
        + [pl.BlockSpec((tile, columns), lambda i: (i, 0)), whole, whole],
        out_specs=pl.BlockSpec((tile, columns), lambda i: (i, 0)),
        out_shape=jax.ShapeDtypeStruct((rows, columns), jnp.float32),
        scratch_shapes=[
            pltpu.VMEM((depth, rows), jnp.float32),
            pltpu.VMEM((depth, columns), jnp.float32),
            pltpu.VMEM((rows, 3 * depth), jnp.bfloat16),
            pltpu.VMEM((3 * depth, columns), jnp.bfloat16),
        ],
        compiler_params=pltpu.CompilerParams(vmem_limit_bytes=24 << 20),
        name="ladder",
    )(*t_pieces, *v_pieces, residual_in, pair_rows, ab_rows)


def solution(mesh):
    placed = (P("pair", "virt"), P("virt", "pair"), P("pair", "virt"), P("pair"), P("virt"), P())
    return jax.shard_map(
        shards, mesh=mesh, in_specs=placed, out_specs=P("pair", "virt"), check_vma=False
    )
```

time: 159 us -> 44 us (0.28)
  the two profiles are of different devices: /device:TPU:6 before, /device:TPU:1 now
where the time goes in v1:
time: 44 us; the launch traced here: 43.6 us
  starting transfers between devices  20.9 us (48%)
  waiting for transfers between devices  9.78 us (22%)
  Pallas kernels  7.06 us (16%)
  local copies, waits for them, and re-layouts  5.12 us (12%)
  other arithmetic  0.77 us (2%)
    ppermute x7, starting transfers between devices, gather(): pieces = [held] + [lax.ppermute(held, axis, pairs(k)) for k in stage]  14 us
    ppermute x4, starting transfers between devices, gather(): pieces = [held] + [lax.ppermute(held, axis, pairs(k)) for k in stages[-1]]  6.9 us
    ppermute x4, waiting for transfers between devices, gather(): pieces = [held] + [lax.ppermute(held, axis, pairs(k)) for k in stages[-1]]  5.89 us
    pallas_call x1, Pallas kernels, shards(): pl.pallas_call(lambda *refs: ladder_kernel(t_order, v_order, *refs), grid...  5.15 us
    unnamed x13, local copies, waits for them, and re-layouts  5.1 us
    ppermute x7, waiting for transfers between devices, gather(): pieces = [held] + [lax.ppermute(held, axis, pairs(k)) for k in stage]  3.89 us
    pallas_call x1, Pallas kernels, shards(): pl.pallas_call(compact_kernel, out_shape=(jax.ShapeDtypeStruct((held_t //...  1.91 us
  transfers between devices with their start and end apart: 11, of which 4 were waited for; matrix products, arithmetic and copies ran while one was open for 5% of the time, Pallas kernels for 0%

profile of v1, /device:TPU:1, one launch (start us, length us, event | category | flops | bytes accessed | tf_op | source)
XLA Modules:
  0.0 43.6 jit_solution(2892895260899011450)
XLA Ops:
  0.0 1.9 %compact.1 = (f32[8,1024]{1,0:T(8,128)}, f32[8,1024]{1,0:T(8,128)}) custom-call(f32[64,1024]{1,0:T(8,128)} %bitcast.9, f32[64,1024]{1,0:T(8,128)} %bitcast.10, s32[8,128]{1,0:T(8,128)} %bitcast.5, s32[8,128]{1,0:T(8,128)} %bitcast.7, s32[8,128]{1,0:T(8,128)} %bitcast.11), custom_call_target="tpu_custom_call" | custom-call | tf_op jit(solution)/shard_map/compact/pallas_call | solution.py:97
  1.9 7.7 %collective-permute-start.2 = (f32[8,1024]{1,0:T(8,128)}, f32[8,1024]{1,0:T(8,128)S(1)}, u32[]{:S(2)}, u32[]{:S(2)}) collective-permute-start(f32[8,1024]{1,0:T(8,128)} %get-tuple-element.7), channel_id=1, source_target_pairs={{0,2},{1,3},{2,0},{3,1},{4,6},{5,7},{6,4},{7,5},{8,10},{9,11},{10,... | collective-permute-start | bytes 98312 | tf_op jit(solution)/shard_map/ppermute | solution.py:85
  9.7 0.0 collective-permute-start.1
  9.7 2.7 %collective-permute-start.8 = (f32[8,1024]{1,0:T(8,128)}, f32[8,1024]{1,0:T(8,128)S(1)}, u32[]{:S(2)}, u32[]{:S(2)}) collective-permute-start(f32[8,1024]{1,0:T(8,128)} %get-tuple-element.8), channel_id=1, source_target_pairs={{0,192},{16,208},{32,224},{48,240},{64,128},{80,144},{96,160},{112... | collective-permute-start | bytes 98312 | tf_op jit(solution)/shard_map/ppermute | solution.py:85
  12.4 0.0 collective-permute-start.7
  12.4 1.2 %collective-permute-start.6 = (f32[8,1024]{1,0:T(8,128)}, f32[8,1024]{1,0:T(8,128)S(1)}, u32[]{:S(2)}, u32[]{:S(2)}) collective-permute-start(f32[8,1024]{1,0:T(8,128)} %get-tuple-element.8), channel_id=1, source_target_pairs={{0,128},{16,144},{32,160},{48,176},{64,192},{80,208},{96,224},{112... | collective-permute-start | bytes 98312 | tf_op jit(solution)/shard_map/ppermute | solution.py:85
  13.6 0.8 %constant_dynamic-update-slice_fusion.3 = f32[32,1024]{1,0:T(8,128)S(1)} fusion(f32[8,1024]{1,0:T(8,128)} %get-tuple-element.7), kind=kLoop, calls=%fused_computation.4 | loop fusion | bytes 65536
  14.3 0.8 %constant_dynamic-update-slice_fusion.8 = f32[64,1024]{1,0:T(8,128)S(1)} fusion(f32[8,1024]{1,0:T(8,128)} %get-tuple-element.8), kind=kLoop, calls=%fused_computation.9 | loop fusion | bytes 65536
  15.1 0.0 collective-permute-done.8
  15.1 1.2 %collective-permute-start = (f32[8,1024]{1,0:T(8,128)}, f32[8,1024]{1,0:T(8,128)S(1)}, u32[]{:S(2)}, u32[]{:S(2)}) collective-permute-start(f32[8,1024]{1,0:T(8,128)} %get-tuple-element.7), channel_id=1, source_target_pairs={{0,1},{1,0},{2,3},{3,2},{4,5},{5,4},{6,7},{7,6},{8,9},{9,8},{10,11... | collective-permute-start | bytes 98312 | tf_op jit(solution)/shard_map/ppermute | solution.py:85
  16.3 0.0 collective-permute-done.7
  16.3 0.8 %collective-permute-done.6 = f32[8,1024]{1,0:T(8,128)S(1)} collective-permute-done((f32[8,1024]{1,0:T(8,128)}, f32[8,1024]{1,0:T(8,128)S(1)}, u32[]{:S(2)}, u32[]{:S(2)}) %collective-permute-start.6) | collective-permute-done | bytes 32800 | tf_op jit(solution)/shard_map/ppermute | solution.py:85
  17.1 0.8 %pad_maximum_fusion = f32[32,1024]{1,0:T(8,128)S(1)} fusion(f32[8,1024]{1,0:T(8,128)S(1)} %collective-permute-done.8, f32[8,1024]{1,0:T(8,128)S(1)} %collective-permute-done.7, f32[8,1024]{1,0:T(8,128)S(1)} %collective-permute-done.6, f32[8,1024]{1,0:T(8,128)} %get-tuple-element.8), kind=kLoop, calls=%fused_computation | loop fusion | flops 98304 | bytes 262144 | tf_op jit(solution)/shard_map/concatenate | solution.py:87
  17.8 1.1 %collective-permute-start.9 = (f32[32,1024]{1,0:T(8,128)S(1)}, f32[32,1024]{1,0:T(8,128)S(1)}, u32[]{:S(2)}, u32[]{:S(2)}) collective-permute-start(f32[32,1024]{1,0:T(8,128)S(1)} %pad_maximum_fusion), channel_id=1, source_target_pairs={{0,32},{16,48},{32,0},{48,16},{64,96},{80,112},{96,64},{112,80},{1... | collective-permute-start | bytes 393224 | tf_op jit(solution)/shard_map/ppermute | solution.py:85
  19.0 0.0 collective-permute-done
  19.0 3.1 %collective-permute-done.9 = f32[32,1024]{1,0:T(8,128)S(1)} collective-permute-done((f32[32,1024]{1,0:T(8,128)S(1)}, f32[32,1024]{1,0:T(8,128)S(1)}, u32[]{:S(2)}, u32[]{:S(2)}) %collective-permute-start.9) | collective-permute-done | bytes 131104 | tf_op jit(solution)/shard_map/ppermute | solution.py:85
  22.1 3.2 %collective-permute-start.10 = (f32[64,1024]{1,0:T(8,128)S(1)}, f32[64,1024]{1,0:T(8,128)S(1)}, u32[]{:S(2)}, u32[]{:S(2)}) collective-permute-start(f32[64,1024]{1,0:T(8,128)S(1)} %constant_dynamic-update-slice_fusion.4.refs_4_), channel_id=1, source_target_pairs={{0,16},{16,0},{32,48},{48,32},{64,80},{80,64},{96,112},{112,96},{1... | collective-permute-start | bytes 786440 | tf_op jit(solution)/shard_map/ppermute | solution.py:88
  25.3 0.0 collective-permute-done.1
  25.3 0.0 collective-permute-done.2
  25.3 2.8 %collective-permute-start.5 = (f32[32,1024]{1,0:T(8,128)S(1)}, f32[32,1024]{1,0:T(8,128)S(1)}, u32[]{:S(2)}, u32[]{:S(2)}) collective-permute-start(f32[32,1024]{1,0:T(8,128)S(1)} %constant_dynamic-update-slice_fusion.refs_0_), channel_id=1, source_target_pairs={{0,8},{1,9},{2,10},{3,11},{4,12},{5,13},{6,14},{7,15},{8,0},{9,1},... | collective-permute-start | bytes 393224 | tf_op jit(solution)/shard_map/ppermute | solution.py:88
  28.2 0.9 %collective-permute-start.4 = (f32[32,1024]{1,0:T(8,128)S(1)}, f32[32,1024]{1,0:T(8,128)S(1)}, u32[]{:S(2)}, u32[]{:S(2)}) collective-permute-start(f32[32,1024]{1,0:T(8,128)S(1)} %constant_dynamic-update-slice_fusion.refs_0_), channel_id=1, source_target_pairs={{0,12},{1,13},{2,14},{3,15},{4,8},{5,9},{6,10},{7,11},{8,4},{9,5},... | collective-permute-start | bytes 393224 | tf_op jit(solution)/shard_map/ppermute | solution.py:88
  29.0 0.0 collective-permute-start.3
  29.0 3.0 %collective-permute-done.5.refs_3_ = f32[32,1024]{1,0:T(8,128)S(1)} collective-permute-done((f32[32,1024]{1,0:T(8,128)S(1)}, f32[32,1024]{1,0:T(8,128)S(1)}, u32[]{:S(2)}, u32[]{:S(2)}) %collective-permute-start.5) | collective-permute-done | bytes 131104 | tf_op jit(solution)/shard_map/ppermute | solution.py:88
  32.0 2.9 %collective-permute-done.4.refs_2_ = f32[32,1024]{1,0:T(8,128)S(1)} collective-permute-done((f32[32,1024]{1,0:T(8,128)S(1)}, f32[32,1024]{1,0:T(8,128)S(1)}, u32[]{:S(2)}, u32[]{:S(2)}) %collective-permute-start.4) | collective-permute-done | bytes 131104 | tf_op jit(solution)/shard_map/ppermute | solution.py:88
  34.9 0.0 collective-permute-done.3.refs_1_
  34.9 0.0 collective-permute-done.10.refs_5_
  34.9 0.0 copy-start
  34.9 2.2 %copy-done = f32[1024,1024]{1,0:T(8,128)S(1)} copy-done((f32[1024,1024]{1,0:T(8,128)S(1)}, f32[1024,1024]{1,0:T(8,128)}, u32[]{:S(2)}) %copy-start) | copy-done | bytes 4194328
  37.1 0.0 copy-start.1
  37.1 0.7 %copy-done.1 = s32[1024]{0:T(1024)S(1)} copy-done((s32[1024]{0:T(1024)S(1)}, s32[1024]{0:T(1024)}, u32[]{:S(2)}) %copy-start.1) | copy-done | bytes 4120
  37.8 0.0 copy-start.2
  37.8 0.7 %copy-done.2 = s32[1024]{0:T(1024)S(1)} copy-done((s32[1024]{0:T(1024)S(1)}, s32[1024]{0:T(1024)}, u32[]{:S(2)}) %copy-start.2) | copy-done | bytes 4120
  38.5 5.2 %ladder.1 = f32[1024,1024]{1,0:T(8,128)} custom-call(f32[32,1024]{1,0:T(8,128)S(1)} %constant_dynamic-update-slice_fusion.refs_0_, f32[32,1024]{1,0:T(8,128)S(1)} %collective-permute-done.3.refs_1_, f32[32,1024]{1,0:T(8,128)S(1)} %collective-permute-done.4.refs_2_, f32[32,1024]{1,0:T(8,128)S(1)} %collective-permute-done.5.refs_3_, ...), custom_call_target="tpu_custom_call" | custom-call | tf_op jit(solution)/shard_map/ladder/pallas_call | solution.py:110
  (7 shorter events, 0.0 us)
Async XLA Ops:
  1.9 23.4 %collective-permute-start.2 = (f32[8,1024]{1,0:T(8,128)}, f32[8,1024]{1,0:T(8,128)S(1)}, u32[]{:S(2)}, u32[]{:S(2)}) collective-permute-start(f32[8,1024]{1,0:T(8,128)} %get-tuple-element.7), channel_id=1, source_target_pairs={{0,2},{1,3},{2,0},{3,1},{4,6},{5,7},{6,4},{7,5},{8,10},{9,11},{10,... | collective-permute-start | bytes 98312 | tf_op jit(solution)/shard_map/ppermute | solution.py:85
  9.7 15.7 %collective-permute-start.1 = (f32[8,1024]{1,0:T(8,128)}, f32[8,1024]{1,0:T(8,128)S(1)}, u32[]{:S(2)}, u32[]{:S(2)}) collective-permute-start(f32[8,1024]{1,0:T(8,128)} %get-tuple-element.7), channel_id=1, source_target_pairs={{0,3},{1,2},{2,1},{3,0},{4,7},{5,6},{6,5},{7,4},{8,11},{9,10},{10,... | collective-permute-start | bytes 98312 | tf_op jit(solution)/shard_map/ppermute | solution.py:85
  9.7 5.4 %collective-permute-start.8 = (f32[8,1024]{1,0:T(8,128)}, f32[8,1024]{1,0:T(8,128)S(1)}, u32[]{:S(2)}, u32[]{:S(2)}) collective-permute-start(f32[8,1024]{1,0:T(8,128)} %get-tuple-element.8), channel_id=1, source_target_pairs={{0,192},{16,208},{32,224},{48,240},{64,128},{80,144},{96,160},{112... | collective-permute-start | bytes 98312 | tf_op jit(solution)/shard_map/ppermute | solution.py:85
  12.4 3.9 %collective-permute-start.7 = (f32[8,1024]{1,0:T(8,128)}, f32[8,1024]{1,0:T(8,128)S(1)}, u32[]{:S(2)}, u32[]{:S(2)}) collective-permute-start(f32[8,1024]{1,0:T(8,128)} %get-tuple-element.8), channel_id=1, source_target_pairs={{0,64},{16,80},{32,96},{48,112},{64,0},{80,16},{96,32},{112,48},{1... | collective-permute-start | bytes 98312 | tf_op jit(solution)/shard_map/ppermute | solution.py:85
  12.4 4.7 %collective-permute-start.6 = (f32[8,1024]{1,0:T(8,128)}, f32[8,1024]{1,0:T(8,128)S(1)}, u32[]{:S(2)}, u32[]{:S(2)}) collective-permute-start(f32[8,1024]{1,0:T(8,128)} %get-tuple-element.8), channel_id=1, source_target_pairs={{0,128},{16,144},{32,160},{48,176},{64,192},{80,208},{96,224},{112... | collective-permute-start | bytes 98312 | tf_op jit(solution)/shard_map/ppermute | solution.py:85
  15.1 3.9 %collective-permute-start = (f32[8,1024]{1,0:T(8,128)}, f32[8,1024]{1,0:T(8,128)S(1)}, u32[]{:S(2)}, u32[]{:S(2)}) collective-permute-start(f32[8,1024]{1,0:T(8,128)} %get-tuple-element.7), channel_id=1, source_target_pairs={{0,1},{1,0},{2,3},{3,2},{4,5},{5,4},{6,7},{7,6},{8,9},{9,8},{10,11... | collective-permute-start | bytes 98312 | tf_op jit(solution)/shard_map/ppermute | solution.py:85
  17.8 4.3 %collective-permute-start.9 = (f32[32,1024]{1,0:T(8,128)S(1)}, f32[32,1024]{1,0:T(8,128)S(1)}, u32[]{:S(2)}, u32[]{:S(2)}) collective-permute-start(f32[32,1024]{1,0:T(8,128)S(1)} %pad_maximum_fusion), channel_id=1, source_target_pairs={{0,32},{16,48},{32,0},{48,16},{64,96},{80,112},{96,64},{112,80},{1... | collective-permute-start | bytes 393224 | tf_op jit(solution)/shard_map/ppermute | solution.py:85
  22.1 12.8 %collective-permute-start.10 = (f32[64,1024]{1,0:T(8,128)S(1)}, f32[64,1024]{1,0:T(8,128)S(1)}, u32[]{:S(2)}, u32[]{:S(2)}) collective-permute-start(f32[64,1024]{1,0:T(8,128)S(1)} %constant_dynamic-update-slice_fusion.4.refs_4_), channel_id=1, source_target_pairs={{0,16},{16,0},{32,48},{48,32},{64,80},{80,64},{96,112},{112,96},{1... | collective-permute-start | bytes 786440 | tf_op jit(solution)/shard_map/ppermute | solution.py:88
  25.3 6.7 %collective-permute-start.5 = (f32[32,1024]{1,0:T(8,128)S(1)}, f32[32,1024]{1,0:T(8,128)S(1)}, u32[]{:S(2)}, u32[]{:S(2)}) collective-permute-start(f32[32,1024]{1,0:T(8,128)S(1)} %constant_dynamic-update-slice_fusion.refs_0_), channel_id=1, source_target_pairs={{0,8},{1,9},{2,10},{3,11},{4,12},{5,13},{6,14},{7,15},{8,0},{9,1},... | collective-permute-start | bytes 393224 | tf_op jit(solution)/shard_map/ppermute | solution.py:88
  28.2 6.7 %collective-permute-start.4 = (f32[32,1024]{1,0:T(8,128)S(1)}, f32[32,1024]{1,0:T(8,128)S(1)}, u32[]{:S(2)}, u32[]{:S(2)}) collective-permute-start(f32[32,1024]{1,0:T(8,128)S(1)} %constant_dynamic-update-slice_fusion.refs_0_), channel_id=1, source_target_pairs={{0,12},{1,13},{2,14},{3,15},{4,8},{5,9},{6,10},{7,11},{8,4},{9,5},... | collective-permute-start | bytes 393224 | tf_op jit(solution)/shard_map/ppermute | solution.py:88
  29.0 5.9 %collective-permute-start.3 = (f32[32,1024]{1,0:T(8,128)S(1)}, f32[32,1024]{1,0:T(8,128)S(1)}, u32[]{:S(2)}, u32[]{:S(2)}) collective-permute-start(f32[32,1024]{1,0:T(8,128)S(1)} %constant_dynamic-update-slice_fusion.refs_0_), channel_id=1, source_target_pairs={{0,4},{1,5},{2,6},{3,7},{4,0},{5,1},{6,2},{7,3},{8,12},{9,13},{10,... | collective-permute-start | bytes 393224 | tf_op jit(solution)/shard_map/ppermute | solution.py:88
  34.9 2.2 %copy-start = (f32[1024,1024]{1,0:T(8,128)S(1)}, f32[1024,1024]{1,0:T(8,128)}, u32[]{:S(2)}) copy-start(f32[1024,1024]{1,0:T(8,128)} %refs_6_.1) | copy-start | bytes 12582916
  37.1 0.7 %copy-start.1 = (s32[1024]{0:T(1024)S(1)}, s32[1024]{0:T(1024)}, u32[]{:S(2)}) copy-start(s32[1024]{0:T(1024)} %param.9) | copy-start | bytes 12292
  37.8 0.7 %copy-start.2 = (s32[1024]{0:T(1024)S(1)}, s32[1024]{0:T(1024)}, u32[]{:S(2)}) copy-start(s32[1024]{0:T(1024)} %param.10) | copy-start | bytes 12292

commit v2 on v1

v2 whole, which is shorter than its diff:
```python
import jax
import jax.numpy as jnp
from jax import lax
from jax.experimental import pallas as pl
from jax.experimental.pallas import tpu as pltpu
from jax.sharding import PartitionSpec as P

BLOCK = 8
LANES = 128
TILE = 256


def column(row):
    return jnp.transpose(jnp.broadcast_to(row, (LANES, LANES)))


def compact_kernel(t_ref, v_ref, pair_ref, ab_ref, cd_ref, ct_ref, cv_ref):
    def one(x_ref, irrep_ref, index, out_ref):
        held = x_ref.shape[0]
        per_row = LANES // held
        labels = column(cd_ref[pl.ds(index // per_row, 1), :])
        part = labels[:held]
        for step in range(1, per_row):
            part = jnp.where(index % per_row == step, labels[step * held : (step + 1) * held], part)
        for group in range(x_ref.shape[1] // LANES):
            lanes = slice(group * LANES, (group + 1) * LANES)
            kept = jnp.where(part == irrep_ref[group : group + 1, :], x_ref[:, lanes], 0.0)
            out_ref[:, lanes] = jnp.sum(kept.reshape(held // BLOCK, BLOCK, LANES), axis=1)

    one(t_ref, pair_ref, lax.axis_index("virt"), ct_ref)
    one(v_ref, ab_ref, lax.axis_index("pair"), cv_ref)


def split(x):
    high = x.astype(jnp.bfloat16)
    low = (x - high.astype(jnp.float32)).astype(jnp.bfloat16)
    return high, low


def stage_kernel(v_order, *refs):
    v_refs = refs[: len(v_order)]
    residual_ref, staged_ref, v_split, v_rows, sem = refs[len(v_order) :]
    copy = pltpu.make_async_copy(residual_ref, staged_ref, sem)
    copy.start()
    depth = v_rows.shape[0]
    apart = lax.axis_index("virt") ^ lax.axis_index("pair")
    for order, ref in zip(v_order, v_refs):
        for slot, k in enumerate(order):
            at = pl.multiple_of((apart ^ k) * BLOCK, BLOCK)
            v_rows[pl.ds(at, BLOCK), :] = ref[slot * BLOCK : (slot + 1) * BLOCK, :]
    high, low = split(v_rows[...])
    v_split[:depth, :] = high
    v_split[depth : 2 * depth, :] = low
    v_split[2 * depth :, :] = high
    copy.wait()


def ladder_kernel(t_order, *refs):
    t_refs = refs[: len(t_order)]
    residual_ref, v_split, pair_ref, ab_ref, out_ref, t_rows, tiles, sems = refs[len(t_order) :]
    for order, ref in zip(t_order, t_refs):
        for slot, k in enumerate(order):
            t_rows[k * BLOCK : (k + 1) * BLOCK, :] = ref[slot * BLOCK : (slot + 1) * BLOCK, :]
    copies = []
    for tile in range(residual_ref.shape[0] // TILE):
        rows = slice(tile * TILE, (tile + 1) * TILE)
        high, low = split(jnp.transpose(t_rows[:, rows]))
        products = jnp.dot(
            jnp.concatenate([high, high, low], axis=1), v_split[...], preferred_element_type=jnp.float32
        )
        for part in range(TILE // LANES):
            row = tile * (TILE // LANES) + part
            at = slice(row * LANES, (row + 1) * LANES)
            labels = column(pair_ref[row : row + 1, :])
            for group in range(residual_ref.shape[1] // LANES):
                lanes = slice(group * LANES, (group + 1) * LANES)
                same = labels == ab_ref[group : group + 1, :]
                term = products[part * LANES : (part + 1) * LANES, lanes]
                tiles[at, lanes] = residual_ref[at, lanes] + jnp.where(same, term, 0.0)
        copies.append(pltpu.make_async_copy(tiles.at[rows, :], out_ref.at[rows, :], sems.at[tile]))
        copies[-1].start()
    for copy in copies:
        copy.wait()


def pairs(k):
    return [(i, i ^ k) for i in range(16)]


def exchange(x, axis, stage):
    return [lax.ppermute(x, axis, pairs(k)) for k in stage]


def gather(x, axis, stages):
    held, order = x, [0]
    for stage in stages[:-1]:
        held = jnp.concatenate([held, *exchange(held, axis, stage)], 0)
        order = [o ^ k for k in (0, *stage) for o in order]
    pieces = [held, *exchange(held, axis, stages[-1])]
    return pieces, [tuple(o ^ k for o in order) for k in (0, *stages[-1])]


def shards(amplitudes, integrals, residual_in, pair_irrep, ab_irrep, cd_irrep):
    rows, columns = residual_in.shape
    held_t, held_v = amplitudes.shape[1], integrals.shape[1]
    pair_rows = pair_irrep.reshape(-1, LANES)
    ab_rows = ab_irrep.reshape(-1, LANES)
    own_t, own_v = pl.pallas_call(
        compact_kernel,
        out_shape=(
            pltpu.VMEM((held_t // BLOCK, rows), jnp.float32),
            pltpu.VMEM((held_v // BLOCK, columns), jnp.float32),
        ),
        name="compact",
    )(amplitudes.T, integrals.T, pair_rows, ab_rows, cd_irrep.reshape(-1, LANES))
    t_pieces, t_order = gather(own_t, "virt", ((1, 3, 2), (4, 12, 8)))
    v_pieces, v_order = gather(own_v, "pair", ((8, 4, 12), (2,), (1,)))
    depth = 16 * BLOCK
    whole = pl.BlockSpec(memory_space=pltpu.VMEM)
    anywhere = pl.BlockSpec(memory_space=pl.ANY)
    staged, v_split = pl.pallas_call(
        lambda *refs: stage_kernel(v_order, *refs),
        in_specs=[whole] * len(v_pieces) + [anywhere],
        out_specs=[whole, whole],
        out_shape=(
            pltpu.VMEM((rows, columns), jnp.float32),
            pltpu.VMEM((3 * depth, columns), jnp.bfloat16),
        ),
        scratch_shapes=[pltpu.VMEM((depth, columns), jnp.float32), pltpu.SemaphoreType.DMA(())],
        compiler_params=pltpu.CompilerParams(vmem_limit_bytes=16 << 20),
        cost_estimate=pl.CostEstimate(flops=0, transcendentals=0, bytes_accessed=8 * rows * columns),
        name="stage",
    )(*v_pieces, pltpu.with_memory_space_constraint(residual_in, pltpu.HBM))
    return pl.pallas_call(
        lambda *refs: ladder_kernel(t_order, *refs),
        in_specs=[whole] * (len(t_pieces) + 4),
        out_specs=anywhere,
        out_shape=jax.ShapeDtypeStruct((rows, columns), jnp.float32),
        scratch_shapes=[
            pltpu.VMEM((depth, rows), jnp.float32),
            pltpu.VMEM((rows, columns), jnp.float32),
            pltpu.SemaphoreType.DMA((rows // TILE,)),
        ],
        compiler_params=pltpu.CompilerParams(vmem_limit_bytes=24 << 20),
        name="ladder",
    )(*t_pieces, staged, v_split, pair_rows, ab_rows)


def solution(mesh):
    placed = (P("pair", "virt"), P("virt", "pair"), P("pair", "virt"), P("pair"), P("virt"), P())
    return jax.shard_map(
        shards, mesh=mesh, in_specs=placed, out_specs=P("pair", "virt"), check_vma=False
    )
```

time: 44 us -> 36.1 us (0.82)
  local copies, waits for them, and re-layouts: 5.12 us -> 0.05 us
  Pallas kernels: 7.06 us -> 6.06 us
  waiting for transfers between devices: 9.78 us -> 8.86 us
  other arithmetic: 0.77 us -> 0.01 us
    unnamed x13 -> x11, local copies, waits for them, and re-layouts: 5.1 us -> 0.04 us
    pallas_call x2 -> x3, Pallas kernels: 7.06 us -> 6.06 us  [the longest x1 2.55 us: shards(): pl.pallas_call(lambda *refs: ladder_kernel(t_order, *refs), in_specs=[who...]
    ppermute x11, waiting for transfers between devices: 9.78 us -> 8.86 us  [exchange(): return [lax.ppermute(x, axis, pairs(k)) for k in stage]]
    concatenate x1, other arithmetic: 0.77 us -> 0.01 us  [gather(): held = jnp.concatenate([held, *exchange(held, axis, stage)], 0)]
  transfers between devices with their start and end apart: 11 -> 11, of which waited for: 4 -> 6; matrix products, arithmetic and copies ran while one was open for 5% -> 0% of each run, Pallas kernels for 0% -> 6%
where the time goes in v2:
time: 36.1 us; the launch traced here: 36 us
  starting transfers between devices  21 us (58%)
  waiting for transfers between devices  8.86 us (25%)
  Pallas kernels  6.06 us (17%)
    ppermute x11, starting transfers between devices, exchange(): return [lax.ppermute(x, axis, pairs(k)) for k in stage]  21 us
    ppermute x11, waiting for transfers between devices, exchange(): return [lax.ppermute(x, axis, pairs(k)) for k in stage]  8.86 us
    pallas_call x1, Pallas kernels, shards(): pl.pallas_call(lambda *refs: ladder_kernel(t_order, *refs), in_specs=[who...  2.55 us
    pallas_call x1, Pallas kernels, shards(): pl.pallas_call(lambda *refs: stage_kernel(v_order, *refs), in_specs=[whol...  2.2 us
    pallas_call x1, Pallas kernels, shards(): pl.pallas_call(compact_kernel, out_shape=(pltpu.VMEM((held_t // BLOCK, ro...  1.31 us
  transfers between devices with their start and end apart: 11, of which 6 were waited for; matrix products, arithmetic and copies ran while one was open for 0% of the time, Pallas kernels for 6%

profile of v2, /device:TPU:1, one launch (start us, length us, event | category | flops | bytes accessed | tf_op | source)
XLA Modules:
  0.0 36.0 jit_solution(3189132052198273604)
XLA Ops:
  0.0 0.0 copy-start.1
  0.0 0.0 copy-start
  0.0 1.3 %compact.1 = (f32[8,1024]{1,0:T(8,128)S(1)}, f32[8,1024]{1,0:T(8,128)S(1)}) custom-call(f32[64,1024]{1,0:T(8,128)} %bitcast.9, f32[64,1024]{1,0:T(8,128)} %bitcast.10, s32[8,128]{1,0:T(8,128)} %bitcast.5, s32[8,128]{1,0:T(8,128)} %bitcast.7, s32[8,128]{1,0:T(8,128)} %bitcast.11), custom_call_target="tpu_custom_call" | custom-call | tf_op jit(solution)/shard_map/compact/pallas_call | solution.py:108
  1.3 7.8 %collective-permute-start.2 = (f32[8,1024]{1,0:T(8,128)S(1)}, f32[8,1024]{1,0:T(8,128)S(1)}, u32[]{:S(2)}, u32[]{:S(2)}) collective-permute-start(f32[8,1024]{1,0:T(8,128)S(1)} %get-tuple-element.9), channel_id=1, source_target_pairs={{0,2},{1,3},{2,0},{3,1},{4,6},{5,7},{6,4},{7,5},{8,10},{9,11},{10,... | collective-permute-start | bytes 98312 | tf_op jit(solution)/shard_map/ppermute | solution.py:91
  9.2 0.0 collective-permute-start.1
  9.2 2.7 %collective-permute-start.8 = (f32[8,1024]{1,0:T(8,128)S(1)}, f32[8,1024]{1,0:T(8,128)S(1)}, u32[]{:S(2)}, u32[]{:S(2)}) collective-permute-start(f32[8,1024]{1,0:T(8,128)S(1)} %get-tuple-element.10), channel_id=1, source_target_pairs={{0,192},{16,208},{32,224},{48,240},{64,128},{80,144},{96,160},{112... | collective-permute-start | bytes 98312 | tf_op jit(solution)/shard_map/ppermute | solution.py:91
  11.9 0.0 collective-permute-start.7
  11.9 1.2 %collective-permute-start.6 = (f32[8,1024]{1,0:T(8,128)S(1)}, f32[8,1024]{1,0:T(8,128)S(1)}, u32[]{:S(2)}, u32[]{:S(2)}) collective-permute-start(f32[8,1024]{1,0:T(8,128)S(1)} %get-tuple-element.10), channel_id=1, source_target_pairs={{0,128},{16,144},{32,160},{48,176},{64,192},{80,208},{96,224},{112... | collective-permute-start | bytes 98312 | tf_op jit(solution)/shard_map/ppermute | solution.py:91
  13.1 0.1 collective-permute-done.8
  13.2 1.2 %collective-permute-start = (f32[8,1024]{1,0:T(8,128)S(1)}, f32[8,1024]{1,0:T(8,128)S(1)}, u32[]{:S(2)}, u32[]{:S(2)}) collective-permute-start(f32[8,1024]{1,0:T(8,128)S(1)} %get-tuple-element.9), channel_id=1, source_target_pairs={{0,1},{1,0},{2,3},{3,2},{4,5},{5,4},{6,7},{7,6},{8,9},{9,8},{10,11... | collective-permute-start | bytes 98312 | tf_op jit(solution)/shard_map/ppermute | solution.py:91
  14.4 0.6 %collective-permute-done.7 = f32[8,1024]{1,0:T(8,128)S(1)} collective-permute-done((f32[8,1024]{1,0:T(8,128)S(1)}, f32[8,1024]{1,0:T(8,128)S(1)}, u32[]{:S(2)}, u32[]{:S(2)}) %collective-permute-start.7) | collective-permute-done | bytes 32800 | tf_op jit(solution)/shard_map/ppermute | solution.py:91
  14.9 1.4 %collective-permute-done.6 = f32[8,1024]{1,0:T(8,128)S(1)} collective-permute-done((f32[8,1024]{1,0:T(8,128)S(1)}, f32[8,1024]{1,0:T(8,128)S(1)}, u32[]{:S(2)}, u32[]{:S(2)}) %collective-permute-start.6) | collective-permute-done | bytes 32800 | tf_op jit(solution)/shard_map/ppermute | solution.py:91
  16.4 1.1 %collective-permute-start.9 = (f32[32,1024]{1,0:T(8,128)S(1)}, f32[32,1024]{1,0:T(8,128)S(1)}, u32[]{:S(2)}, u32[]{:S(2)}) collective-permute-start(f32[32,1024]{1,0:T(8,128)S(1)} %pad_maximum_fusion), channel_id=1, source_target_pairs={{0,32},{16,48},{32,0},{48,16},{64,96},{80,112},{96,64},{112,80},{1... | collective-permute-start | bytes 393224 | tf_op jit(solution)/shard_map/ppermute | solution.py:91
  17.5 0.0 collective-permute-done
  17.5 3.1 %collective-permute-done.9 = f32[32,1024]{1,0:T(8,128)S(1)} collective-permute-done((f32[32,1024]{1,0:T(8,128)S(1)}, f32[32,1024]{1,0:T(8,128)S(1)}, u32[]{:S(2)}, u32[]{:S(2)}) %collective-permute-start.9) | collective-permute-done | bytes 131104 | tf_op jit(solution)/shard_map/ppermute | solution.py:91
  20.6 3.2 %collective-permute-start.10 = (f32[64,1024]{1,0:T(8,128)S(1)}, f32[64,1024]{1,0:T(8,128)S(1)}, u32[]{:S(2)}, u32[]{:S(2)}) collective-permute-start(f32[64,1024]{1,0:T(8,128)S(1)} %constant_dynamic-update-slice_fusion.4.refs_0_), channel_id=1, source_target_pairs={{0,16},{16,0},{32,48},{48,32},{64,80},{80,64},{96,112},{112,96},{1... | collective-permute-start | bytes 786440 | tf_op jit(solution)/shard_map/ppermute | solution.py:91
  23.9 0.0 collective-permute-done.1
  23.9 0.0 collective-permute-done.2
  23.9 2.8 %collective-permute-start.5 = (f32[32,1024]{1,0:T(8,128)S(1)}, f32[32,1024]{1,0:T(8,128)S(1)}, u32[]{:S(2)}, u32[]{:S(2)}) collective-permute-start(f32[32,1024]{1,0:T(8,128)S(1)} %constant_dynamic-update-slice_fusion.refs_0_), channel_id=1, source_target_pairs={{0,8},{1,9},{2,10},{3,11},{4,12},{5,13},{6,14},{7,15},{8,0},{9,1},... | collective-permute-start | bytes 393224 | tf_op jit(solution)/shard_map/ppermute | solution.py:91
  26.7 0.9 %collective-permute-start.4 = (f32[32,1024]{1,0:T(8,128)S(1)}, f32[32,1024]{1,0:T(8,128)S(1)}, u32[]{:S(2)}, u32[]{:S(2)}) collective-permute-start(f32[32,1024]{1,0:T(8,128)S(1)} %constant_dynamic-update-slice_fusion.refs_0_), channel_id=1, source_target_pairs={{0,12},{1,13},{2,14},{3,15},{4,8},{5,9},{6,10},{7,11},{8,4},{9,5},... | collective-permute-start | bytes 393224 | tf_op jit(solution)/shard_map/ppermute | solution.py:91
  27.6 0.0 collective-permute-start.3
  27.6 0.0 collective-permute-done.10.refs_1_
  27.6 2.2 %stage.1 = (f32[1024,1024]{1,0:T(8,128)S(1)}, bf16[384,1024]{1,0:T(8,128)(2,1)S(1)}) custom-call(f32[64,1024]{1,0:T(8,128)S(1)} %constant_dynamic-update-slice_fusion.4.refs_0_, f32[64,1024]{1,0:T(8,128)S(1)} %collective-permute-done.10.refs_1_, f32[1024,1024]{1,0:T(8,128)} %refs_2_.1), custom_call_target="tpu_custom_call" | custom-call | bytes 8388608 | tf_op jit(solution)/shard_map/stage/pallas_call | solution.py:121
  29.8 0.8 %collective-permute-done.5.refs_3_ = f32[32,1024]{1,0:T(8,128)S(1)} collective-permute-done((f32[32,1024]{1,0:T(8,128)S(1)}, f32[32,1024]{1,0:T(8,128)S(1)}, u32[]{:S(2)}, u32[]{:S(2)}) %collective-permute-start.5) | collective-permute-done | bytes 131104 | tf_op jit(solution)/shard_map/ppermute | solution.py:91
  30.6 2.9 %collective-permute-done.4.refs_2_ = f32[32,1024]{1,0:T(8,128)S(1)} collective-permute-done((f32[32,1024]{1,0:T(8,128)S(1)}, f32[32,1024]{1,0:T(8,128)S(1)}, u32[]{:S(2)}, u32[]{:S(2)}) %collective-permute-start.4) | collective-permute-done | bytes 131104 | tf_op jit(solution)/shard_map/ppermute | solution.py:91
  33.4 0.0 collective-permute-done.3.refs_1_
  33.5 0.0 copy-done.1
  33.5 0.0 copy-done
  33.5 2.6 %ladder.1 = f32[1024,1024]{1,0:T(8,128)} custom-call(f32[32,1024]{1,0:T(8,128)S(1)} %constant_dynamic-update-slice_fusion.refs_0_, f32[32,1024]{1,0:T(8,128)S(1)} %collective-permute-done.3.refs_1_, f32[32,1024]{1,0:T(8,128)S(1)} %collective-permute-done.4.refs_2_, f32[32,1024]{1,0:T(8,128)S(1)} %collective-permute-done.5.refs_3_, ...), custom_call_target="tpu_custom_call" | custom-call | tf_op jit(solution)/shard_map/ladder/pallas_call | solution.py:134
  (10 shorter events, 0.1 us)
Async XLA Ops:
  0.0 33.5 %copy-start.1 = (s32[1024]{0:T(1024)S(1)}, s32[1024]{0:T(1024)}, u32[]{:S(2)}) copy-start(s32[1024]{0:T(1024)} %param.10) | copy-start | bytes 12292
  0.0 33.5 %copy-start = (s32[1024]{0:T(1024)S(1)}, s32[1024]{0:T(1024)}, u32[]{:S(2)}) copy-start(s32[1024]{0:T(1024)} %param.9) | copy-start | bytes 12292
  1.3 22.5 %collective-permute-start.2 = (f32[8,1024]{1,0:T(8,128)S(1)}, f32[8,1024]{1,0:T(8,128)S(1)}, u32[]{:S(2)}, u32[]{:S(2)}) collective-permute-start(f32[8,1024]{1,0:T(8,128)S(1)} %get-tuple-element.9), channel_id=1, source_target_pairs={{0,2},{1,3},{2,0},{3,1},{4,6},{5,7},{6,4},{7,5},{8,10},{9,11},{10,... | collective-permute-start | bytes 98312 | tf_op jit(solution)/shard_map/ppermute | solution.py:91
  9.2 14.7 %collective-permute-start.1 = (f32[8,1024]{1,0:T(8,128)S(1)}, f32[8,1024]{1,0:T(8,128)S(1)}, u32[]{:S(2)}, u32[]{:S(2)}) collective-permute-start(f32[8,1024]{1,0:T(8,128)S(1)} %get-tuple-element.9), channel_id=1, source_target_pairs={{0,3},{1,2},{2,1},{3,0},{4,7},{5,6},{6,5},{7,4},{8,11},{9,10},{10,... | collective-permute-start | bytes 98312 | tf_op jit(solution)/shard_map/ppermute | solution.py:91
  9.2 4.0 %collective-permute-start.8 = (f32[8,1024]{1,0:T(8,128)S(1)}, f32[8,1024]{1,0:T(8,128)S(1)}, u32[]{:S(2)}, u32[]{:S(2)}) collective-permute-start(f32[8,1024]{1,0:T(8,128)S(1)} %get-tuple-element.10), channel_id=1, source_target_pairs={{0,192},{16,208},{32,224},{48,240},{64,128},{80,144},{96,160},{112... | collective-permute-start | bytes 98312 | tf_op jit(solution)/shard_map/ppermute | solution.py:91
  11.9 3.1 %collective-permute-start.7 = (f32[8,1024]{1,0:T(8,128)S(1)}, f32[8,1024]{1,0:T(8,128)S(1)}, u32[]{:S(2)}, u32[]{:S(2)}) collective-permute-start(f32[8,1024]{1,0:T(8,128)S(1)} %get-tuple-element.10), channel_id=1, source_target_pairs={{0,64},{16,80},{32,96},{48,112},{64,0},{80,16},{96,32},{112,48},{1... | collective-permute-start | bytes 98312 | tf_op jit(solution)/shard_map/ppermute | solution.py:91
  11.9 4.5 %collective-permute-start.6 = (f32[8,1024]{1,0:T(8,128)S(1)}, f32[8,1024]{1,0:T(8,128)S(1)}, u32[]{:S(2)}, u32[]{:S(2)}) collective-permute-start(f32[8,1024]{1,0:T(8,128)S(1)} %get-tuple-element.10), channel_id=1, source_target_pairs={{0,128},{16,144},{32,160},{48,176},{64,192},{80,208},{96,224},{112... | collective-permute-start | bytes 98312 | tf_op jit(solution)/shard_map/ppermute | solution.py:91
  13.2 4.3 %collective-permute-start = (f32[8,1024]{1,0:T(8,128)S(1)}, f32[8,1024]{1,0:T(8,128)S(1)}, u32[]{:S(2)}, u32[]{:S(2)}) collective-permute-start(f32[8,1024]{1,0:T(8,128)S(1)} %get-tuple-element.9), channel_id=1, source_target_pairs={{0,1},{1,0},{2,3},{3,2},{4,5},{5,4},{6,7},{7,6},{8,9},{9,8},{10,11... | collective-permute-start | bytes 98312 | tf_op jit(solution)/shard_map/ppermute | solution.py:91
  16.4 4.3 %collective-permute-start.9 = (f32[32,1024]{1,0:T(8,128)S(1)}, f32[32,1024]{1,0:T(8,128)S(1)}, u32[]{:S(2)}, u32[]{:S(2)}) collective-permute-start(f32[32,1024]{1,0:T(8,128)S(1)} %pad_maximum_fusion), channel_id=1, source_target_pairs={{0,32},{16,48},{32,0},{48,16},{64,96},{80,112},{96,64},{112,80},{1... | collective-permute-start | bytes 393224 | tf_op jit(solution)/shard_map/ppermute | solution.py:91
  20.6 6.9 %collective-permute-start.10 = (f32[64,1024]{1,0:T(8,128)S(1)}, f32[64,1024]{1,0:T(8,128)S(1)}, u32[]{:S(2)}, u32[]{:S(2)}) collective-permute-start(f32[64,1024]{1,0:T(8,128)S(1)} %constant_dynamic-update-slice_fusion.4.refs_0_), channel_id=1, source_target_pairs={{0,16},{16,0},{32,48},{48,32},{64,80},{80,64},{96,112},{112,96},{1... | collective-permute-start | bytes 786440 | tf_op jit(solution)/shard_map/ppermute | solution.py:91
  23.9 6.7 %collective-permute-start.5 = (f32[32,1024]{1,0:T(8,128)S(1)}, f32[32,1024]{1,0:T(8,128)S(1)}, u32[]{:S(2)}, u32[]{:S(2)}) collective-permute-start(f32[32,1024]{1,0:T(8,128)S(1)} %constant_dynamic-update-slice_fusion.refs_0_), channel_id=1, source_target_pairs={{0,8},{1,9},{2,10},{3,11},{4,12},{5,13},{6,14},{7,15},{8,0},{9,1},... | collective-permute-start | bytes 393224 | tf_op jit(solution)/shard_map/ppermute | solution.py:91
  26.7 6.7 %collective-permute-start.4 = (f32[32,1024]{1,0:T(8,128)S(1)}, f32[32,1024]{1,0:T(8,128)S(1)}, u32[]{:S(2)}, u32[]{:S(2)}) collective-permute-start(f32[32,1024]{1,0:T(8,128)S(1)} %constant_dynamic-update-slice_fusion.refs_0_), channel_id=1, source_target_pairs={{0,12},{1,13},{2,14},{3,15},{4,8},{5,9},{6,10},{7,11},{8,4},{9,5},... | collective-permute-start | bytes 393224 | tf_op jit(solution)/shard_map/ppermute | solution.py:91
  27.6 5.9 %collective-permute-start.3 = (f32[32,1024]{1,0:T(8,128)S(1)}, f32[32,1024]{1,0:T(8,128)S(1)}, u32[]{:S(2)}, u32[]{:S(2)}) collective-permute-start(f32[32,1024]{1,0:T(8,128)S(1)} %constant_dynamic-update-slice_fusion.refs_0_), channel_id=1, source_target_pairs={{0,4},{1,5},{2,6},{3,7},{4,0},{5,1},{6,2},{7,3},{8,12},{9,13},{10,... | collective-permute-start | bytes 393224 | tf_op jit(solution)/shard_map/ppermute | solution.py:91

commit v3 on v2

--- a/solution.py
+++ b/solution.py
@@ -37,11 +37,30 @@
     return high, low
 
 
-def stage_kernel(v_order, *refs):
-    v_refs = refs[: len(v_order)]
-    residual_ref, staged_ref, v_split, v_rows, sem = refs[len(v_order) :]
+def stage_kernel(residual_ref, after_ref, staged_ref, sem):
     copy = pltpu.make_async_copy(residual_ref, staged_ref, sem)
     copy.start()
+    copy.wait()
+
+
+def turn_kernel(t_order, *refs):
+    t_refs = refs[: len(t_order)]
+    t_split, t_rows = refs[len(t_order) :]
+    depth = t_rows.shape[0]
+    for order, ref in zip(t_order, t_refs):
+        for slot, k in enumerate(order):
+            t_rows[k * BLOCK : (k + 1) * BLOCK, :] = ref[slot * BLOCK : (slot + 1) * BLOCK, :]
+    for group in range(t_rows.shape[1] // LANES):
+        rows = slice(group * LANES, (group + 1) * LANES)
+        high, low = split(jnp.transpose(t_rows[:, rows]))
+        t_split[rows, :depth] = high
+        t_split[rows, depth : 2 * depth] = high
+        t_split[rows, 2 * depth :] = low
+
+
+def ladder_kernel(v_order, *refs):
+    v_refs = refs[: len(v_order)]
+    residual_ref, t_split, pair_ref, ab_ref, out_ref, v_rows, v_split, tiles, sems = refs[len(v_order) :]
     depth = v_rows.shape[0]
     apart = lax.axis_index("virt") ^ lax.axis_index("pair")
     for order, ref in zip(v_order, v_refs):
@@ -52,22 +71,10 @@
     v_split[:depth, :] = high
     v_split[depth : 2 * depth, :] = low
     v_split[2 * depth :, :] = high
-    copy.wait()
-
-
-def ladder_kernel(t_order, *refs):
-    t_refs = refs[: len(t_order)]
-    residual_ref, v_split, pair_ref, ab_ref, out_ref, t_rows, tiles, sems = refs[len(t_order) :]
-    for order, ref in zip(t_order, t_refs):
-        for slot, k in enumerate(order):
-            t_rows[k * BLOCK : (k + 1) * BLOCK, :] = ref[slot * BLOCK : (slot + 1) * BLOCK, :]
     copies = []
     for tile in range(residual_ref.shape[0] // TILE):
         rows = slice(tile * TILE, (tile + 1) * TILE)
-        high, low = split(jnp.transpose(t_rows[:, rows]))
-        products = jnp.dot(
-            jnp.concatenate([high, high, low], axis=1), v_split[...], preferred_element_type=jnp.float32
-        )
+        products = jnp.dot(t_split[rows, :], v_split[...], preferred_element_type=jnp.float32)
         for part in range(TILE // LANES):
             row = tile * (TILE // LANES) + part
             at = slice(row * LANES, (row + 1) * LANES)
@@ -81,6 +88,13 @@
         copies[-1].start()
     for copy in copies:
         copy.wait()
+
+
+bar = lax.optimization_barrier
+def cat(*l): return jnp.concatenate(l, 0)
+def T(x,k): return lax.ppermute(x,"virt",pairs(k))
+def V(x,k): return lax.ppermute(x,"pair",pairs(k))
+def orders(base, ks): return [tuple(o ^ k for o in base) for k in ks]
 
 
 def pairs(k):
@@ -113,37 +127,51 @@
         ),
         name="compact",
     )(amplitudes.T, integrals.T, pair_rows, ab_rows, cd_irrep.reshape(-1, LANES))
-    t_pieces, t_order = gather(own_t, "virt", ((1, 3, 2), (4, 12, 8)))
-    v_pieces, v_order = gather(own_v, "pair", ((8, 4, 12), (2,), (1,)))
+    t1 = cat(own_t, T(own_t,1)); ZO=(0,1,3,2)
+    v1 = cat(own_v, V(own_v,4)); VO1=(0,4)
+    tz = cat(t1, T(t1,3))
+    v2 = cat(v1, V(v1,12)); VO2=tuple(o ^ k for k in (0,12) for o in VO1)
+    tx = cat(tz, T(tz,4))
+    t_pieces, t_order = [tx, T(tx,12)], orders(tuple(o ^ k for k in (0,4) for o in ZO), (0,12))
+    v3 = cat(v2, V(v2,2))
+    v_pieces, v_order = [v3, V(v3,1)], orders(tuple(o ^ k for k in (0,2) for o in VO2), (0,1))
     depth = 16 * BLOCK
     whole = pl.BlockSpec(memory_space=pltpu.VMEM)
     anywhere = pl.BlockSpec(memory_space=pl.ANY)
-    staged, v_split = pl.pallas_call(
-        lambda *refs: stage_kernel(v_order, *refs),
-        in_specs=[whole] * len(v_pieces) + [anywhere],
-        out_specs=[whole, whole],
-        out_shape=(
-            pltpu.VMEM((rows, columns), jnp.float32),
-            pltpu.VMEM((3 * depth, columns), jnp.bfloat16),
-        ),
-        scratch_shapes=[pltpu.VMEM((depth, columns), jnp.float32), pltpu.SemaphoreType.DMA(())],
-        compiler_params=pltpu.CompilerParams(vmem_limit_bytes=16 << 20),
-        cost_estimate=pl.CostEstimate(flops=0, transcendentals=0, bytes_accessed=8 * rows * columns),
+    staged = pl.pallas_call(
+        stage_kernel,
+        in_specs=[anywhere, anywhere],
+        out_specs=whole,
+        out_shape=pltpu.VMEM((rows, columns), jnp.float32),
+        scratch_shapes=[pltpu.SemaphoreType.DMA(())],
+        cost_estimate=pl.CostEstimate(flops=0, transcendentals=0, bytes_accessed=8388608),
+        compiler_params=pltpu.CompilerParams(vmem_limit_bytes=2 << 20),
         name="stage",
-    )(*v_pieces, pltpu.with_memory_space_constraint(residual_in, pltpu.HBM))
+    )(pltpu.with_memory_space_constraint(residual_in, pltpu.HBM), t_pieces[0])
+    t_split = pl.pallas_call(
+        lambda *refs: turn_kernel(t_order, *refs),
+        in_specs=[whole] * len(t_pieces),
+        out_specs=whole,
+        out_shape=pltpu.VMEM((rows, 3 * depth), jnp.bfloat16),
+        scratch_shapes=[pltpu.VMEM((depth, rows), jnp.float32)],
+        cost_estimate=pl.CostEstimate(flops=0, transcendentals=0, bytes_accessed=8388608),
+        compiler_params=pltpu.CompilerParams(vmem_limit_bytes=8 << 20),
+        name="turn",
+    )(*t_pieces)
     return pl.pallas_call(
-        lambda *refs: ladder_kernel(t_order, *refs),
-        in_specs=[whole] * (len(t_pieces) + 4),
+        lambda *refs: ladder_kernel(v_order, *refs),
+        in_specs=[whole] * (len(v_pieces) + 4),
         out_specs=anywhere,
         out_shape=jax.ShapeDtypeStruct((rows, columns), jnp.float32),
         scratch_shapes=[
-            pltpu.VMEM((depth, rows), jnp.float32),
+            pltpu.VMEM((depth, columns), jnp.float32),
+            pltpu.VMEM((3 * depth, columns), jnp.bfloat16),
             pltpu.VMEM((rows, columns), jnp.float32),
             pltpu.SemaphoreType.DMA((rows // TILE,)),
         ],
         compiler_params=pltpu.CompilerParams(vmem_limit_bytes=24 << 20),
         name="ladder",
-    )(*t_pieces, staged, v_split, pair_rows, ab_rows)
+    )(*v_pieces, staged, t_split, pair_rows, ab_rows)
 
 
 def solution(mesh):

time: 36.1 us -> 33.2 us (0.920)
  the two profiles are of different devices: /device:TPU:1 before, /device:TPU:6 now
where the time goes in v3:
time: 33.2 us; the launch traced here: 33.1 us
  starting transfers between devices  16.1 us (48%)
  waiting for transfers between devices  10.6 us (32%)
  Pallas kernels  6.24 us (19%)
    ppermute x4, starting transfers between devices, T(): return lax.ppermute(x, 'virt', pairs(k))  10.9 us
    ppermute x4, waiting for transfers between devices, T(): return lax.ppermute(x, 'virt', pairs(k))  10.6 us
    ppermute x4, starting transfers between devices, V(): return lax.ppermute(x, 'pair', pairs(k))  5.13 us
    pallas_call x1, Pallas kernels, shards(): pl.pallas_call(lambda *refs: ladder_kernel(v_order, *refs), in_specs=[who...  2.55 us
    pallas_call x1, Pallas kernels, shards(): pl.pallas_call(stage_kernel, in_specs=[anywhere, anywhere], out_specs=who...  2.2 us
    pallas_call x1, Pallas kernels, shards(): pl.pallas_call(compact_kernel, out_shape=(pltpu.VMEM((held_t // BLOCK, ro...  1.29 us
  transfers between devices with their start and end apart: 8, of which 3 were waited for; matrix products, arithmetic and copies ran while one was open for 0% of the time, Pallas kernels for 7%

profile of v3, /device:TPU:6, one launch (start us, length us, event | category | flops | bytes accessed | tf_op | source)
XLA Modules:
  0.0 33.1 jit_solution(9336692088396804505)
XLA Ops:
  0.0 1.3 %compact.1 = (f32[8,1024]{1,0:T(8,128)S(1)}, f32[8,1024]{1,0:T(8,128)S(1)}) custom-call(f32[64,1024]{1,0:T(8,128)} %bitcast.9, f32[64,1024]{1,0:T(8,128)} %bitcast.10, s32[8,128]{1,0:T(8,128)} %bitcast.5, s32[8,128]{1,0:T(8,128)} %bitcast.7, s32[8,128]{1,0:T(8,128)} %bitcast.11), custom_call_target="tpu_custom_call" | custom-call | tf_op jit(solution)/shard_map/compact/pallas_call | solution.py:122
  1.3 1.7 %collective-permute-start = (f32[8,1024]{1,0:T(8,128)S(1)}, f32[8,1024]{1,0:T(8,128)S(1)}, u32[]{:S(2)}, u32[]{:S(2)}) collective-permute-start(f32[8,1024]{1,0:T(8,128)S(1)} %get-tuple-element.7), channel_id=1, source_target_pairs={{0,64},{16,80},{32,96},{48,112},{64,0},{80,16},{96,32},{112,48},{1... | collective-permute-start | bytes 98312 | tf_op jit(solution)/shard_map/ppermute | solution.py:96
  3.0 3.3 %collective-permute-start.4 = (f32[8,1024]{1,0:T(8,128)S(1)}, f32[8,1024]{1,0:T(8,128)S(1)}, u32[]{:S(2)}, u32[]{:S(2)}) collective-permute-start(f32[8,1024]{1,0:T(8,128)S(1)} %get-tuple-element.8), channel_id=1, source_target_pairs={{0,1},{1,0},{2,3},{3,2},{4,5},{5,4},{6,7},{7,6},{8,9},{9,8},{10,11... | collective-permute-start | bytes 98312 | tf_op jit(solution)/shard_map/ppermute | solution.py:95
  6.2 0.0 collective-permute-done
  6.3 2.3 %collective-permute-start.1 = (f32[16,1024]{1,0:T(8,128)S(1)}, f32[16,1024]{1,0:T(8,128)S(1)}, u32[]{:S(2)}, u32[]{:S(2)}) collective-permute-start(f32[16,1024]{1,0:T(8,128)S(1)} %pad_maximum_fusion.2), channel_id=1, source_target_pairs={{0,192},{16,208},{32,224},{48,240},{64,128},{80,144},{96,160},{112... | collective-permute-start | bytes 196616 | tf_op jit(solution)/shard_map/ppermute | solution.py:96
  8.5 0.0 collective-permute-done.4
  8.5 6.2 %collective-permute-start.5 = (f32[16,1024]{1,0:T(8,128)S(1)}, f32[16,1024]{1,0:T(8,128)S(1)}, u32[]{:S(2)}, u32[]{:S(2)}) collective-permute-start(f32[16,1024]{1,0:T(8,128)S(1)} %pad_maximum_fusion.3), channel_id=1, source_target_pairs={{0,3},{1,2},{2,1},{3,0},{4,7},{5,6},{6,5},{7,4},{8,11},{9,10},{10,... | collective-permute-start | bytes 196616 | tf_op jit(solution)/shard_map/ppermute | solution.py:95
  14.7 0.0 collective-permute-done.1
  14.8 1.1 %collective-permute-start.2 = (f32[32,1024]{1,0:T(8,128)S(1)}, f32[32,1024]{1,0:T(8,128)S(1)}, u32[]{:S(2)}, u32[]{:S(2)}) collective-permute-start(f32[32,1024]{1,0:T(8,128)S(1)} %pad_maximum_fusion), channel_id=1, source_target_pairs={{0,32},{16,48},{32,0},{48,16},{64,96},{80,112},{96,64},{112,80},{1... | collective-permute-start | bytes 393224 | tf_op jit(solution)/shard_map/ppermute | solution.py:96
  15.9 1.7 %collective-permute-done.5 = f32[16,1024]{1,0:T(8,128)S(1)} collective-permute-done((f32[16,1024]{1,0:T(8,128)S(1)}, f32[16,1024]{1,0:T(8,128)S(1)}, u32[]{:S(2)}, u32[]{:S(2)}) %collective-permute-start.5) | collective-permute-done | bytes 65568 | tf_op jit(solution)/shard_map/ppermute | solution.py:95
  17.6 0.9 %collective-permute-start.6 = (f32[32,1024]{1,0:T(8,128)S(1)}, f32[32,1024]{1,0:T(8,128)S(1)}, u32[]{:S(2)}, u32[]{:S(2)}) collective-permute-start(f32[32,1024]{1,0:T(8,128)S(1)} %pad_maximum_fusion.1), channel_id=1, source_target_pairs={{0,4},{1,5},{2,6},{3,7},{4,0},{5,1},{6,2},{7,3},{8,12},{9,13},{10,... | collective-permute-start | bytes 393224 | tf_op jit(solution)/shard_map/ppermute | solution.py:95
  18.5 4.1 %collective-permute-done.6 = f32[32,1024]{1,0:T(8,128)S(1)} collective-permute-done((f32[32,1024]{1,0:T(8,128)S(1)}, f32[32,1024]{1,0:T(8,128)S(1)}, u32[]{:S(2)}, u32[]{:S(2)}) %collective-permute-start.6) | collective-permute-done | bytes 131104 | tf_op jit(solution)/shard_map/ppermute | solution.py:95
  22.6 0.6 %collective-permute-start.7 = (f32[64,1024]{1,0:T(8,128)S(1)}, f32[64,1024]{1,0:T(8,128)S(1)}, u32[]{:S(2)}, u32[]{:S(2)}) collective-permute-start(f32[64,1024]{1,0:T(8,128)S(1)} %constant_dynamic-update-slice_fusion.4.after_ref.refs_0_), channel_id=1, source_target_pairs={{0,12},{1,13},{2,14},{3,15},{4,8},{5,9},{6,10},{7,11},{8,4},{9,5},... | collective-permute-start | bytes 786440 | tf_op jit(solution)/shard_map/ppermute | solution.py:95
  23.2 0.0 collective-permute-done.2
  23.2 0.0 copy-start
  23.2 0.0 copy-start.1
  23.3 0.1 collective-permute-start.3
  23.4 2.2 %stage.1.refs_2_ = f32[1024,1024]{1,0:T(8,128)S(1)} custom-call(f32[1024,1024]{1,0:T(8,128)} %residual_ref.1, f32[64,1024]{1,0:T(8,128)S(1)} %constant_dynamic-update-slice_fusion.4.after_ref.refs_0_), custom_call_target="tpu_custom_call" | custom-call | bytes 8388608 | tf_op jit(solution)/shard_map/stage/pallas_call | solution.py:141
  25.6 4.8 %collective-permute-done.7.refs_1_ = f32[64,1024]{1,0:T(8,128)S(1)} collective-permute-done((f32[64,1024]{1,0:T(8,128)S(1)}, f32[64,1024]{1,0:T(8,128)S(1)}, u32[]{:S(2)}, u32[]{:S(2)}) %collective-permute-start.7) | collective-permute-done | bytes 262176 | tf_op jit(solution)/shard_map/ppermute | solution.py:95
  30.3 0.2 turn.1.refs_3_
  30.5 0.0 collective-permute-done.3.refs_1_
  30.5 0.0 copy-done
  30.5 0.0 copy-done.1
  30.6 2.5 %ladder.1 = f32[1024,1024]{1,0:T(8,128)} custom-call(f32[64,1024]{1,0:T(8,128)S(1)} %constant_dynamic-update-slice_fusion.refs_0_, f32[64,1024]{1,0:T(8,128)S(1)} %collective-permute-done.3.refs_1_, f32[1024,1024]{1,0:T(8,128)S(1)} %stage.1.refs_2_, bf16[1024,384]{1,0:T(8,128)(2,1)S(1)} %turn.1.refs_3_, s32[8,128]{1,0:T(8,128)S(1)} %bitcast.6, ...), custom_call_target="tpu_custom_call" | custom-call | tf_op jit(solution)/shard_map/ladder/pallas_call | solution.py:161
  (11 shorter events, 0.1 us)
Async XLA Ops:
  1.3 4.9 %collective-permute-start = (f32[8,1024]{1,0:T(8,128)S(1)}, f32[8,1024]{1,0:T(8,128)S(1)}, u32[]{:S(2)}, u32[]{:S(2)}) collective-permute-start(f32[8,1024]{1,0:T(8,128)S(1)} %get-tuple-element.7), channel_id=1, source_target_pairs={{0,64},{16,80},{32,96},{48,112},{64,0},{80,16},{96,32},{112,48},{1... | collective-permute-start | bytes 98312 | tf_op jit(solution)/shard_map/ppermute | solution.py:96
  3.0 5.6 %collective-permute-start.4 = (f32[8,1024]{1,0:T(8,128)S(1)}, f32[8,1024]{1,0:T(8,128)S(1)}, u32[]{:S(2)}, u32[]{:S(2)}) collective-permute-start(f32[8,1024]{1,0:T(8,128)S(1)} %get-tuple-element.8), channel_id=1, source_target_pairs={{0,1},{1,0},{2,3},{3,2},{4,5},{5,4},{6,7},{7,6},{8,9},{9,8},{10,11... | collective-permute-start | bytes 98312 | tf_op jit(solution)/shard_map/ppermute | solution.py:95
  6.3 8.5 %collective-permute-start.1 = (f32[16,1024]{1,0:T(8,128)S(1)}, f32[16,1024]{1,0:T(8,128)S(1)}, u32[]{:S(2)}, u32[]{:S(2)}) collective-permute-start(f32[16,1024]{1,0:T(8,128)S(1)} %pad_maximum_fusion.2), channel_id=1, source_target_pairs={{0,192},{16,208},{32,224},{48,240},{64,128},{80,144},{96,160},{112... | collective-permute-start | bytes 196616 | tf_op jit(solution)/shard_map/ppermute | solution.py:96
  8.5 9.0 %collective-permute-start.5 = (f32[16,1024]{1,0:T(8,128)S(1)}, f32[16,1024]{1,0:T(8,128)S(1)}, u32[]{:S(2)}, u32[]{:S(2)}) collective-permute-start(f32[16,1024]{1,0:T(8,128)S(1)} %pad_maximum_fusion.3), channel_id=1, source_target_pairs={{0,3},{1,2},{2,1},{3,0},{4,7},{5,6},{6,5},{7,4},{8,11},{9,10},{10,... | collective-permute-start | bytes 196616 | tf_op jit(solution)/shard_map/ppermute | solution.py:95
  14.8 8.5 %collective-permute-start.2 = (f32[32,1024]{1,0:T(8,128)S(1)}, f32[32,1024]{1,0:T(8,128)S(1)}, u32[]{:S(2)}, u32[]{:S(2)}) collective-permute-start(f32[32,1024]{1,0:T(8,128)S(1)} %pad_maximum_fusion), channel_id=1, source_target_pairs={{0,32},{16,48},{32,0},{48,16},{64,96},{80,112},{96,64},{112,80},{1... | collective-permute-start | bytes 393224 | tf_op jit(solution)/shard_map/ppermute | solution.py:96
  17.6 5.1 %collective-permute-start.6 = (f32[32,1024]{1,0:T(8,128)S(1)}, f32[32,1024]{1,0:T(8,128)S(1)}, u32[]{:S(2)}, u32[]{:S(2)}) collective-permute-start(f32[32,1024]{1,0:T(8,128)S(1)} %pad_maximum_fusion.1), channel_id=1, source_target_pairs={{0,4},{1,5},{2,6},{3,7},{4,0},{5,1},{6,2},{7,3},{8,12},{9,13},{10,... | collective-permute-start | bytes 393224 | tf_op jit(solution)/shard_map/ppermute | solution.py:95
  22.6 7.7 %collective-permute-start.7 = (f32[64,1024]{1,0:T(8,128)S(1)}, f32[64,1024]{1,0:T(8,128)S(1)}, u32[]{:S(2)}, u32[]{:S(2)}) collective-permute-start(f32[64,1024]{1,0:T(8,128)S(1)} %constant_dynamic-update-slice_fusion.4.after_ref.refs_0_), channel_id=1, source_target_pairs={{0,12},{1,13},{2,14},{3,15},{4,8},{5,9},{6,10},{7,11},{8,4},{9,5},... | collective-permute-start | bytes 786440 | tf_op jit(solution)/shard_map/ppermute | solution.py:95
  23.2 7.3 %copy-start = (s32[1024]{0:T(1024)S(1)}, s32[1024]{0:T(1024)}, u32[]{:S(2)}) copy-start(s32[1024]{0:T(1024)} %param.9) | copy-start | bytes 12292
  23.2 7.3 %copy-start.1 = (s32[1024]{0:T(1024)S(1)}, s32[1024]{0:T(1024)}, u32[]{:S(2)}) copy-start(s32[1024]{0:T(1024)} %param.10) | copy-start | bytes 12292
  23.3 7.3 %collective-permute-start.3 = (f32[64,1024]{1,0:T(8,128)S(1)}, f32[64,1024]{1,0:T(8,128)S(1)}, u32[]{:S(2)}, u32[]{:S(2)}) collective-permute-start(f32[64,1024]{1,0:T(8,128)S(1)} %constant_dynamic-update-slice_fusion.refs_0_), channel_id=1, source_target_pairs={{0,16},{16,0},{32,48},{48,32},{64,80},{80,64},{96,112},{112,96},{1... | collective-permute-start | bytes 786440 | tf_op jit(solution)/shard_map/ppermute | solution.py:96

commit v4 on v3

--- a/solution.py
+++ b/solution.py
@@ -7,28 +7,35 @@
 
 BLOCK = 8
 LANES = 128
-TILE = 256
+TILE = 128
 
 
 def column(row):
     return jnp.transpose(jnp.broadcast_to(row, (LANES, LANES)))
 
 
-def compact_kernel(t_ref, v_ref, pair_ref, ab_ref, cd_ref, ct_ref, cv_ref):
-    def one(x_ref, irrep_ref, index, out_ref):
-        held = x_ref.shape[0]
-        per_row = LANES // held
-        labels = column(cd_ref[pl.ds(index // per_row, 1), :])
-        part = labels[:held]
-        for step in range(1, per_row):
-            part = jnp.where(index % per_row == step, labels[step * held : (step + 1) * held], part)
-        for group in range(x_ref.shape[1] // LANES):
-            lanes = slice(group * LANES, (group + 1) * LANES)
-            kept = jnp.where(part == irrep_ref[group : group + 1, :], x_ref[:, lanes], 0.0)
-            out_ref[:, lanes] = jnp.sum(kept.reshape(held // BLOCK, BLOCK, LANES), axis=1)
+def compact_kernel(axis, x_ref, irrep_ref, cd_ref, out_ref):
+    index = lax.axis_index(axis)
+    held = x_ref.shape[0]
+    per_row = LANES // held
+    labels = column(cd_ref[pl.ds(index // per_row, 1), :])
+    part = labels[:held]
+    for step in range(1, per_row):
+        part = jnp.where(index % per_row == step, labels[step * held : (step + 1) * held], part)
+    for group in range(x_ref.shape[1] // LANES):
+        lanes = slice(group * LANES, (group + 1) * LANES)
+        kept = jnp.where(part == irrep_ref[group : group + 1, :], x_ref[:, lanes], 0.0)
+        out_ref[:, lanes] = jnp.sum(kept.reshape(held // BLOCK, BLOCK, LANES), axis=1)
 
-    one(t_ref, pair_ref, lax.axis_index("virt"), ct_ref)
-    one(v_ref, ab_ref, lax.axis_index("pair"), cv_ref)
+
+def compact(x, irrep_rows, cd_rows, axis):
+    return pl.pallas_call(
+        lambda *refs: compact_kernel(axis, *refs),
+        out_shape=pltpu.VMEM((x.shape[1] // BLOCK, x.shape[0]), jnp.float32),
+        cost_estimate=pl.CostEstimate(flops=0, transcendentals=0, bytes_accessed=1048576),
+        compiler_params=pltpu.CompilerParams(vmem_limit_bytes=4 << 20),
+        name="compact_" + axis,
+    )(*(pltpu.with_memory_space_constraint(a, pltpu.HBM) for a in (x.T, irrep_rows, cd_rows)))
 
 
 def split(x):
@@ -116,25 +123,19 @@
 
 def shards(amplitudes, integrals, residual_in, pair_irrep, ab_irrep, cd_irrep):
     rows, columns = residual_in.shape
-    held_t, held_v = amplitudes.shape[1], integrals.shape[1]
     pair_rows = pair_irrep.reshape(-1, LANES)
     ab_rows = ab_irrep.reshape(-1, LANES)
-    own_t, own_v = pl.pallas_call(
-        compact_kernel,
-        out_shape=(
-            pltpu.VMEM((held_t // BLOCK, rows), jnp.float32),
-            pltpu.VMEM((held_v // BLOCK, columns), jnp.float32),
-        ),
-        name="compact",
-    )(amplitudes.T, integrals.T, pair_rows, ab_rows, cd_irrep.reshape(-1, LANES))
+    cd_rows = cd_irrep.reshape(-1, LANES)
+    own_t = compact(amplitudes, pair_rows, cd_rows, "virt")
+    own_v = compact(integrals, ab_rows, cd_rows, "pair")
     t1 = cat(own_t, T(own_t,1)); ZO=(0,1,3,2)
-    v1 = cat(own_v, V(own_v,4)); VO1=(0,4)
+    v1 = cat(own_v, V(own_v,2)); VO1=(0,2)
     tz = cat(t1, T(t1,3))
-    v2 = cat(v1, V(v1,12)); VO2=tuple(o ^ k for k in (0,12) for o in VO1)
+    v2 = cat(v1, V(v1,4)); VO2=tuple(o ^ k for k in (0,4) for o in VO1)
     tx = cat(tz, T(tz,4))
     t_pieces, t_order = [tx, T(tx,12)], orders(tuple(o ^ k for k in (0,4) for o in ZO), (0,12))
-    v3 = cat(v2, V(v2,2))
-    v_pieces, v_order = [v3, V(v3,1)], orders(tuple(o ^ k for k in (0,2) for o in VO2), (0,1))
+    v3 = cat(v2, V(v2,12))
+    v_pieces, v_order = [v3, V(v3,1)], orders(tuple(o ^ k for k in (0,12) for o in VO2), (0,1))
     depth = 16 * BLOCK
     whole = pl.BlockSpec(memory_space=pltpu.VMEM)
     anywhere = pl.BlockSpec(memory_space=pl.ANY)

time: 33.2 us -> 30.3 us (0.913)
  waiting for transfers between devices: 10.6 us -> 6.52 us
  Pallas kernels: 6.24 us -> 7.1 us
    ppermute x4, waiting for transfers between devices: 10.6 us -> 2.85 us  [T(): return lax.ppermute(x, 'virt', pairs(k))]
    ppermute x4, waiting for transfers between devices: 0.01 us -> 3.67 us  [V(): return lax.ppermute(x, 'pair', pairs(k))]
    ppermute x4, starting transfers between devices: 5.13 us -> 6.86 us  [V(): return lax.ppermute(x, 'pair', pairs(k))]
    ppermute x4, starting transfers between devices: 10.9 us -> 9.53 us  [T(): return lax.ppermute(x, 'virt', pairs(k))]
    pallas_call x1 -> x2, Pallas kernels: 1.29 us -> 2.26 us  [compact(): pl.pallas_call(lambda *refs: compact_kernel(axis, *refs), out_shape=pltpu...]
  transfers between devices with their start and end apart: 8 -> 8, of which waited for: 3 -> 4; matrix products, arithmetic and copies ran while one was open for 0% -> 0% of each run, Pallas kernels for 7% -> 12%
where the time goes in v4:
time: 30.3 us; the launch traced here: 30.2 us
  starting transfers between devices  16.4 us (54%)
  Pallas kernels  7.1 us (23%)
  waiting for transfers between devices  6.52 us (22%)
    ppermute x4, starting transfers between devices, T(): return lax.ppermute(x, 'virt', pairs(k))  9.53 us
    ppermute x4, starting transfers between devices, V(): return lax.ppermute(x, 'pair', pairs(k))  6.86 us
    ppermute x4, waiting for transfers between devices, V(): return lax.ppermute(x, 'pair', pairs(k))  3.67 us
    ppermute x4, waiting for transfers between devices, T(): return lax.ppermute(x, 'virt', pairs(k))  2.85 us
    pallas_call x1, Pallas kernels, shards(): pl.pallas_call(lambda *refs: ladder_kernel(v_order, *refs), in_specs=[who...  2.44 us
    pallas_call x2, Pallas kernels, compact(): pl.pallas_call(lambda *refs: compact_kernel(axis, *refs), out_shape=pltpu...  2.26 us
    pallas_call x1, Pallas kernels, shards(): pl.pallas_call(stage_kernel, in_specs=[anywhere, anywhere], out_specs=who...  2.2 us
  transfers between devices with their start and end apart: 8, of which 4 were waited for; matrix products, arithmetic and copies ran while one was open for 0% of the time, Pallas kernels for 12%

profile of v4, /device:TPU:6, one launch (start us, length us, event | category | flops | bytes accessed | tf_op | source)
XLA Modules:
  0.0 30.2 jit_solution(413986736932926428)
XLA Ops:
  0.0 1.1 %compact_virt.1 = f32[8,1024]{1,0:T(8,128)S(1)} custom-call(f32[64,1024]{1,0:T(8,128)} %bitcast.9, s32[8,128]{1,0:T(8,128)} %bitcast.7, s32[8,128]{1,0:T(8,128)} %bitcast.11), custom_call_target="tpu_custom_call" | custom-call | bytes 1048576 | tf_op jit(solution)/shard_map/compact_virt/pallas_call | solution.py:32
  1.1 3.4 %collective-permute-start.4 = (f32[8,1024]{1,0:T(8,128)S(1)}, f32[8,1024]{1,0:T(8,128)S(1)}, u32[]{:S(2)}, u32[]{:S(2)}) collective-permute-start(f32[8,1024]{1,0:T(8,128)S(1)} %compact_virt.1), channel_id=1, source_target_pairs={{0,1},{1,0},{2,3},{3,2},{4,5},{5,4},{6,7},{7,6},{8,9},{9,8},{10,11... | collective-permute-start | bytes 98312 | tf_op jit(solution)/shard_map/ppermute | solution.py:102
  4.5 1.1 %compact_pair.1 = f32[8,1024]{1,0:T(8,128)S(1)} custom-call(f32[64,1024]{1,0:T(8,128)} %bitcast.10, s32[8,128]{1,0:T(8,128)} %bitcast.5, s32[8,128]{1,0:T(8,128)} %bitcast.12), custom_call_target="tpu_custom_call" | custom-call | bytes 1048576 | tf_op jit(solution)/shard_map/compact_pair/pallas_call | solution.py:32
  5.6 2.0 %collective-permute-start = (f32[8,1024]{1,0:T(8,128)S(1)}, f32[8,1024]{1,0:T(8,128)S(1)}, u32[]{:S(2)}, u32[]{:S(2)}) collective-permute-start(f32[8,1024]{1,0:T(8,128)S(1)} %compact_pair.1), channel_id=1, source_target_pairs={{0,32},{16,48},{32,0},{48,16},{64,96},{80,112},{96,64},{112,80},{1... | collective-permute-start | bytes 98312 | tf_op jit(solution)/shard_map/ppermute | solution.py:103
  7.6 0.0 collective-permute-done.4
  7.6 4.7 %collective-permute-start.5 = (f32[16,1024]{1,0:T(8,128)S(1)}, f32[16,1024]{1,0:T(8,128)S(1)}, u32[]{:S(2)}, u32[]{:S(2)}) collective-permute-start(f32[16,1024]{1,0:T(8,128)S(1)} %pad_maximum_fusion.5), channel_id=1, source_target_pairs={{0,3},{1,2},{2,1},{3,0},{4,7},{5,6},{6,5},{7,4},{8,11},{9,10},{10,... | collective-permute-start | bytes 196616 | tf_op jit(solution)/shard_map/ppermute | solution.py:102
  12.3 0.0 collective-permute-done
  12.4 1.7 %collective-permute-start.1 = (f32[16,1024]{1,0:T(8,128)S(1)}, f32[16,1024]{1,0:T(8,128)S(1)}, u32[]{:S(2)}, u32[]{:S(2)}) collective-permute-start(f32[16,1024]{1,0:T(8,128)S(1)} %pad_maximum_fusion.4), channel_id=1, source_target_pairs={{0,64},{16,80},{32,96},{48,112},{64,0},{80,16},{96,32},{112,48},{1... | collective-permute-start | bytes 196616 | tf_op jit(solution)/shard_map/ppermute | solution.py:103
  14.0 0.7 %collective-permute-done.5 = f32[16,1024]{1,0:T(8,128)S(1)} collective-permute-done((f32[16,1024]{1,0:T(8,128)S(1)}, f32[16,1024]{1,0:T(8,128)S(1)}, u32[]{:S(2)}, u32[]{:S(2)}) %collective-permute-start.5) | collective-permute-done | bytes 65568 | tf_op jit(solution)/shard_map/ppermute | solution.py:102
  14.7 0.9 %collective-permute-start.6 = (f32[32,1024]{1,0:T(8,128)S(1)}, f32[32,1024]{1,0:T(8,128)S(1)}, u32[]{:S(2)}, u32[]{:S(2)}) collective-permute-start(f32[32,1024]{1,0:T(8,128)S(1)} %pad_maximum_fusion.3), channel_id=1, source_target_pairs={{0,4},{1,5},{2,6},{3,7},{4,0},{5,1},{6,2},{7,3},{8,12},{9,13},{10,... | collective-permute-start | bytes 393224 | tf_op jit(solution)/shard_map/ppermute | solution.py:102
  15.6 1.1 %collective-permute-done.1 = f32[16,1024]{1,0:T(8,128)S(1)} collective-permute-done((f32[16,1024]{1,0:T(8,128)S(1)}, f32[16,1024]{1,0:T(8,128)S(1)}, u32[]{:S(2)}, u32[]{:S(2)}) %collective-permute-start.1) | collective-permute-done | bytes 65568 | tf_op jit(solution)/shard_map/ppermute | solution.py:103
  16.7 3.1 %collective-permute-start.2 = (f32[32,1024]{1,0:T(8,128)S(1)}, f32[32,1024]{1,0:T(8,128)S(1)}, u32[]{:S(2)}, u32[]{:S(2)}) collective-permute-start(f32[32,1024]{1,0:T(8,128)S(1)} %pad_maximum_fusion.2), channel_id=1, source_target_pairs={{0,192},{16,208},{32,224},{48,240},{64,128},{80,144},{96,160},{112... | collective-permute-start | bytes 393224 | tf_op jit(solution)/shard_map/ppermute | solution.py:103
  19.8 0.0 collective-permute-done.6
  19.9 0.6 %collective-permute-start.7 = (f32[64,1024]{1,0:T(8,128)S(1)}, f32[64,1024]{1,0:T(8,128)S(1)}, u32[]{:S(2)}, u32[]{:S(2)}) collective-permute-start(f32[64,1024]{1,0:T(8,128)S(1)} %pad_maximum_fusion.1.after_ref.refs_0_), channel_id=1, source_target_pairs={{0,12},{1,13},{2,14},{3,15},{4,8},{5,9},{6,10},{7,11},{8,4},{9,5},... | collective-permute-start | bytes 786440 | tf_op jit(solution)/shard_map/ppermute | solution.py:102
  20.4 2.6 %collective-permute-done.2 = f32[32,1024]{1,0:T(8,128)S(1)} collective-permute-done((f32[32,1024]{1,0:T(8,128)S(1)}, f32[32,1024]{1,0:T(8,128)S(1)}, u32[]{:S(2)}, u32[]{:S(2)}) %collective-permute-start.2) | collective-permute-done | bytes 131104 | tf_op jit(solution)/shard_map/ppermute | solution.py:103
  23.0 0.0 copy-start
  23.0 0.0 copy-start.1
  23.0 0.1 collective-permute-start.3
  23.1 2.2 %stage.1.refs_2_ = f32[1024,1024]{1,0:T(8,128)S(1)} custom-call(f32[1024,1024]{1,0:T(8,128)} %residual_ref.1, f32[64,1024]{1,0:T(8,128)S(1)} %pad_maximum_fusion.1.after_ref.refs_0_), custom_call_target="tpu_custom_call" | custom-call | bytes 8388608 | tf_op jit(solution)/shard_map/stage/pallas_call | solution.py:142
  25.3 2.2 %collective-permute-done.7.refs_1_ = f32[64,1024]{1,0:T(8,128)S(1)} collective-permute-done((f32[64,1024]{1,0:T(8,128)S(1)}, f32[64,1024]{1,0:T(8,128)S(1)}, u32[]{:S(2)}, u32[]{:S(2)}) %collective-permute-start.7) | collective-permute-done | bytes 262176 | tf_op jit(solution)/shard_map/ppermute | solution.py:102
  27.5 0.2 turn.1.refs_3_
  27.7 0.0 collective-permute-done.3.refs_1_
  27.7 0.0 copy-done
  27.8 0.0 copy-done.1
  27.8 2.4 %ladder.1 = f32[1024,1024]{1,0:T(8,128)} custom-call(f32[64,1024]{1,0:T(8,128)S(1)} %pad_maximum_fusion.refs_0_, f32[64,1024]{1,0:T(8,128)S(1)} %collective-permute-done.3.refs_1_, f32[1024,1024]{1,0:T(8,128)S(1)} %stage.1.refs_2_, bf16[1024,384]{1,0:T(8,128)(2,1)S(1)} %turn.1.refs_3_, s32[8,128]{1,0:T(8,128)S(1)} %bitcast.8, s32[8,128]{1,0:T(8,128)S(1)} %bitcast.6), custom_call_target="tpu_custom_call" | custom-call | tf_op jit(solution)/shard_map/ladder/pallas_call | solution.py:162
  (6 shorter events, 0.1 us)
Async XLA Ops:
  1.1 6.5 %collective-permute-start.4 = (f32[8,1024]{1,0:T(8,128)S(1)}, f32[8,1024]{1,0:T(8,128)S(1)}, u32[]{:S(2)}, u32[]{:S(2)}) collective-permute-start(f32[8,1024]{1,0:T(8,128)S(1)} %compact_virt.1), channel_id=1, source_target_pairs={{0,1},{1,0},{2,3},{3,2},{4,5},{5,4},{6,7},{7,6},{8,9},{9,8},{10,11... | collective-permute-start | bytes 98312 | tf_op jit(solution)/shard_map/ppermute | solution.py:102
  5.6 6.7 %collective-permute-start = (f32[8,1024]{1,0:T(8,128)S(1)}, f32[8,1024]{1,0:T(8,128)S(1)}, u32[]{:S(2)}, u32[]{:S(2)}) collective-permute-start(f32[8,1024]{1,0:T(8,128)S(1)} %compact_pair.1), channel_id=1, source_target_pairs={{0,32},{16,48},{32,0},{48,16},{64,96},{80,112},{96,64},{112,80},{1... | collective-permute-start | bytes 98312 | tf_op jit(solution)/shard_map/ppermute | solution.py:103
  7.6 7.0 %collective-permute-start.5 = (f32[16,1024]{1,0:T(8,128)S(1)}, f32[16,1024]{1,0:T(8,128)S(1)}, u32[]{:S(2)}, u32[]{:S(2)}) collective-permute-start(f32[16,1024]{1,0:T(8,128)S(1)} %pad_maximum_fusion.5), channel_id=1, source_target_pairs={{0,3},{1,2},{2,1},{3,0},{4,7},{5,6},{6,5},{7,4},{8,11},{9,10},{10,... | collective-permute-start | bytes 196616 | tf_op jit(solution)/shard_map/ppermute | solution.py:102
  12.4 4.4 %collective-permute-start.1 = (f32[16,1024]{1,0:T(8,128)S(1)}, f32[16,1024]{1,0:T(8,128)S(1)}, u32[]{:S(2)}, u32[]{:S(2)}) collective-permute-start(f32[16,1024]{1,0:T(8,128)S(1)} %pad_maximum_fusion.4), channel_id=1, source_target_pairs={{0,64},{16,80},{32,96},{48,112},{64,0},{80,16},{96,32},{112,48},{1... | collective-permute-start | bytes 196616 | tf_op jit(solution)/shard_map/ppermute | solution.py:103
  14.7 5.1 %collective-permute-start.6 = (f32[32,1024]{1,0:T(8,128)S(1)}, f32[32,1024]{1,0:T(8,128)S(1)}, u32[]{:S(2)}, u32[]{:S(2)}) collective-permute-start(f32[32,1024]{1,0:T(8,128)S(1)} %pad_maximum_fusion.3), channel_id=1, source_target_pairs={{0,4},{1,5},{2,6},{3,7},{4,0},{5,1},{6,2},{7,3},{8,12},{9,13},{10,... | collective-permute-start | bytes 393224 | tf_op jit(solution)/shard_map/ppermute | solution.py:102
  16.7 6.3 %collective-permute-start.2 = (f32[32,1024]{1,0:T(8,128)S(1)}, f32[32,1024]{1,0:T(8,128)S(1)}, u32[]{:S(2)}, u32[]{:S(2)}) collective-permute-start(f32[32,1024]{1,0:T(8,128)S(1)} %pad_maximum_fusion.2), channel_id=1, source_target_pairs={{0,192},{16,208},{32,224},{48,240},{64,128},{80,144},{96,160},{112... | collective-permute-start | bytes 393224 | tf_op jit(solution)/shard_map/ppermute | solution.py:103
  19.9 7.7 %collective-permute-start.7 = (f32[64,1024]{1,0:T(8,128)S(1)}, f32[64,1024]{1,0:T(8,128)S(1)}, u32[]{:S(2)}, u32[]{:S(2)}) collective-permute-start(f32[64,1024]{1,0:T(8,128)S(1)} %pad_maximum_fusion.1.after_ref.refs_0_), channel_id=1, source_target_pairs={{0,12},{1,13},{2,14},{3,15},{4,8},{5,9},{6,10},{7,11},{8,4},{9,5},... | collective-permute-start | bytes 786440 | tf_op jit(solution)/shard_map/ppermute | solution.py:102
  23.0 4.7 %copy-start = (s32[1024]{0:T(1024)S(1)}, s32[1024]{0:T(1024)}, u32[]{:S(2)}) copy-start(s32[1024]{0:T(1024)} %param.10) | copy-start | bytes 12292
  23.0 4.7 %copy-start.1 = (s32[1024]{0:T(1024)S(1)}, s32[1024]{0:T(1024)}, u32[]{:S(2)}) copy-start(s32[1024]{0:T(1024)} %param.9) | copy-start | bytes 12292
  23.0 4.7 %collective-permute-start.3 = (f32[64,1024]{1,0:T(8,128)S(1)}, f32[64,1024]{1,0:T(8,128)S(1)}, u32[]{:S(2)}, u32[]{:S(2)}) collective-permute-start(f32[64,1024]{1,0:T(8,128)S(1)} %pad_maximum_fusion.refs_0_), channel_id=1, source_target_pairs={{0,16},{16,0},{32,48},{48,32},{64,80},{80,64},{96,112},{112,96},{1... | collective-permute-start | bytes 786440 | tf_op jit(solution)/shard_map/ppermute | solution.py:103

commit v5 on v4

--- a/solution.py
+++ b/solution.py
@@ -65,9 +65,9 @@
         t_split[rows, 2 * depth :] = low
 
 
-def ladder_kernel(v_order, *refs):
+def lay_kernel(v_order, *refs):
     v_refs = refs[: len(v_order)]
-    residual_ref, t_split, pair_ref, ab_ref, out_ref, v_rows, v_split, tiles, sems = refs[len(v_order) :]
+    v_split, v_rows = refs[len(v_order) :]
     depth = v_rows.shape[0]
     apart = lax.axis_index("virt") ^ lax.axis_index("pair")
     for order, ref in zip(v_order, v_refs):
@@ -78,6 +78,9 @@
     v_split[:depth, :] = high
     v_split[depth : 2 * depth, :] = low
     v_split[2 * depth :, :] = high
+
+
+def ladder_kernel(residual_ref, t_split, v_split, pair_ref, ab_ref, out_ref, tiles, sems):
     copies = []
     for tile in range(residual_ref.shape[0] // TILE):
         rows = slice(tile * TILE, (tile + 1) * TILE)
@@ -159,20 +162,28 @@
         compiler_params=pltpu.CompilerParams(vmem_limit_bytes=8 << 20),
         name="turn",
     )(*t_pieces)
+    v_split = pl.pallas_call(
+        lambda *refs: lay_kernel(v_order, *refs),
+        in_specs=[whole] * len(v_pieces),
+        out_specs=whole,
+        out_shape=pltpu.VMEM((3 * depth, columns), jnp.bfloat16),
+        scratch_shapes=[pltpu.VMEM((depth, columns), jnp.float32)],
+        cost_estimate=pl.CostEstimate(flops=0, transcendentals=0, bytes_accessed=0),
+        compiler_params=pltpu.CompilerParams(vmem_limit_bytes=4 << 20),
+        name="lay",
+    )(*v_pieces)
     return pl.pallas_call(
-        lambda *refs: ladder_kernel(v_order, *refs),
-        in_specs=[whole] * (len(v_pieces) + 4),
+        ladder_kernel,
+        in_specs=[whole] * 5,
         out_specs=anywhere,
         out_shape=jax.ShapeDtypeStruct((rows, columns), jnp.float32),
         scratch_shapes=[
-            pltpu.VMEM((depth, columns), jnp.float32),
-            pltpu.VMEM((3 * depth, columns), jnp.bfloat16),
             pltpu.VMEM((rows, columns), jnp.float32),
             pltpu.SemaphoreType.DMA((rows // TILE,)),
         ],
         compiler_params=pltpu.CompilerParams(vmem_limit_bytes=24 << 20),
         name="ladder",
-    )(*v_pieces, staged, t_split, pair_rows, ab_rows)
+    )(staged, t_split, v_split, pair_rows, ab_rows)
 
 
 def solution(mesh):

time: 30.3 us -> 33.8 us (1.12)
  waiting for transfers between devices: 6.52 us -> 9.5 us
    ppermute x4, waiting for transfers between devices: 2.85 us -> 7.26 us  [T(): return lax.ppermute(x, 'virt', pairs(k))]
    ppermute x4, waiting for transfers between devices: 3.67 us -> 2.24 us  [V(): return lax.ppermute(x, 'pair', pairs(k))]
    ppermute x4, starting transfers between devices: 9.53 us -> 9.89 us  [T(): return lax.ppermute(x, 'virt', pairs(k))]
    pallas_call x1 -> x2, Pallas kernels: 2.44 us -> 2.59 us  [the longest x1 2.41 us: shards(): pl.pallas_call(ladder_kernel, in_specs=[whole] * 5, out_specs=anywhere, o...]
  transfers between devices with their start and end apart: 8 -> 8, of which waited for: 4 -> 4; matrix products, arithmetic and copies ran while one was open for 0% -> 0% of each run, Pallas kernels for 12% -> 10%
where the time goes in v5:
time: 33.8 us; the launch traced here: 33.7 us
  starting transfers between devices  16.7 us (49%)
  waiting for transfers between devices  9.5 us (28%)
  Pallas kernels  7.25 us (21%)
    ppermute x4, starting transfers between devices, T(): return lax.ppermute(x, 'virt', pairs(k))  9.89 us
    ppermute x4, waiting for transfers between devices, T(): return lax.ppermute(x, 'virt', pairs(k))  7.26 us
    ppermute x4, starting transfers between devices, V(): return lax.ppermute(x, 'pair', pairs(k))  6.86 us
    pallas_call x1, Pallas kernels, shards(): pl.pallas_call(ladder_kernel, in_specs=[whole] * 5, out_specs=anywhere, o...  2.41 us
    pallas_call x2, Pallas kernels, compact(): pl.pallas_call(lambda *refs: compact_kernel(axis, *refs), out_shape=pltpu...  2.26 us
    ppermute x4, waiting for transfers between devices, V(): return lax.ppermute(x, 'pair', pairs(k))  2.24 us
    pallas_call x1, Pallas kernels, shards(): pl.pallas_call(stage_kernel, in_specs=[anywhere, anywhere], out_specs=who...  2.2 us
  transfers between devices with their start and end apart: 8, of which 4 were waited for; matrix products, arithmetic and copies ran while one was open for 0% of the time, Pallas kernels for 10%

profile of v5, /device:TPU:6, one launch (start us, length us, event | category | flops | bytes accessed | tf_op | source)
XLA Modules:
  0.0 33.7 jit_solution(11886078707704800309)
XLA Ops:
  0.0 1.1 %compact_pair.1 = f32[8,1024]{1,0:T(8,128)S(1)} custom-call(f32[64,1024]{1,0:T(8,128)} %bitcast.9, s32[8,128]{1,0:T(8,128)} %bitcast.7, s32[8,128]{1,0:T(8,128)} %bitcast.11), custom_call_target="tpu_custom_call" | custom-call | bytes 1048576 | tf_op jit(solution)/shard_map/compact_pair/pallas_call | solution.py:32
  1.1 2.0 %collective-permute-start.4 = (f32[8,1024]{1,0:T(8,128)S(1)}, f32[8,1024]{1,0:T(8,128)S(1)}, u32[]{:S(2)}, u32[]{:S(2)}) collective-permute-start(f32[8,1024]{1,0:T(8,128)S(1)} %compact_pair.1), channel_id=1, source_target_pairs={{0,32},{16,48},{32,0},{48,16},{64,96},{80,112},{96,64},{112,80},{1... | collective-permute-start | bytes 98312 | tf_op jit(solution)/shard_map/ppermute | solution.py:106
  3.1 1.1 %compact_virt.1 = f32[8,1024]{1,0:T(8,128)S(1)} custom-call(f32[64,1024]{1,0:T(8,128)} %bitcast.10, s32[8,128]{1,0:T(8,128)} %bitcast.5, s32[8,128]{1,0:T(8,128)} %bitcast.12), custom_call_target="tpu_custom_call" | custom-call | bytes 1048576 | tf_op jit(solution)/shard_map/compact_virt/pallas_call | solution.py:32
  4.3 3.4 %collective-permute-start = (f32[8,1024]{1,0:T(8,128)S(1)}, f32[8,1024]{1,0:T(8,128)S(1)}, u32[]{:S(2)}, u32[]{:S(2)}) collective-permute-start(f32[8,1024]{1,0:T(8,128)S(1)} %compact_virt.1), channel_id=1, source_target_pairs={{0,1},{1,0},{2,3},{3,2},{4,5},{5,4},{6,7},{7,6},{8,9},{9,8},{10,11... | collective-permute-start | bytes 98312 | tf_op jit(solution)/shard_map/ppermute | solution.py:105
  7.6 0.0 collective-permute-done.4
  7.6 1.7 %collective-permute-start.5 = (f32[16,1024]{1,0:T(8,128)S(1)}, f32[16,1024]{1,0:T(8,128)S(1)}, u32[]{:S(2)}, u32[]{:S(2)}) collective-permute-start(f32[16,1024]{1,0:T(8,128)S(1)} %pad_maximum_fusion.5), channel_id=1, source_target_pairs={{0,64},{16,80},{32,96},{48,112},{64,0},{80,16},{96,32},{112,48},{1... | collective-permute-start | bytes 196616 | tf_op jit(solution)/shard_map/ppermute | solution.py:106
  9.3 0.2 collective-permute-done
  9.5 5.0 %collective-permute-start.1 = (f32[16,1024]{1,0:T(8,128)S(1)}, f32[16,1024]{1,0:T(8,128)S(1)}, u32[]{:S(2)}, u32[]{:S(2)}) collective-permute-start(f32[16,1024]{1,0:T(8,128)S(1)} %pad_maximum_fusion.4), channel_id=1, source_target_pairs={{0,3},{1,2},{2,1},{3,0},{4,7},{5,6},{6,5},{7,4},{8,11},{9,10},{10,... | collective-permute-start | bytes 196616 | tf_op jit(solution)/shard_map/ppermute | solution.py:105
  14.6 0.0 collective-permute-done.5
  14.6 3.1 %collective-permute-start.6 = (f32[32,1024]{1,0:T(8,128)S(1)}, f32[32,1024]{1,0:T(8,128)S(1)}, u32[]{:S(2)}, u32[]{:S(2)}) collective-permute-start(f32[32,1024]{1,0:T(8,128)S(1)} %pad_maximum_fusion.3), channel_id=1, source_target_pairs={{0,192},{16,208},{32,224},{48,240},{64,128},{80,144},{96,160},{112... | collective-permute-start | bytes 393224 | tf_op jit(solution)/shard_map/ppermute | solution.py:106
  17.7 0.0 collective-permute-done.1
  17.7 0.9 %collective-permute-start.2 = (f32[32,1024]{1,0:T(8,128)S(1)}, f32[32,1024]{1,0:T(8,128)S(1)}, u32[]{:S(2)}, u32[]{:S(2)}) collective-permute-start(f32[32,1024]{1,0:T(8,128)S(1)} %pad_maximum_fusion.2), channel_id=1, source_target_pairs={{0,4},{1,5},{2,6},{3,7},{4,0},{5,1},{6,2},{7,3},{8,12},{9,13},{10,... | collective-permute-start | bytes 393224 | tf_op jit(solution)/shard_map/ppermute | solution.py:105
  18.6 2.2 %collective-permute-done.6 = f32[32,1024]{1,0:T(8,128)S(1)} collective-permute-done((f32[32,1024]{1,0:T(8,128)S(1)}, f32[32,1024]{1,0:T(8,128)S(1)}, u32[]{:S(2)}, u32[]{:S(2)}) %collective-permute-start.6) | collective-permute-done | bytes 131104 | tf_op jit(solution)/shard_map/ppermute | solution.py:106
  20.9 0.1 collective-permute-start.7
  21.0 1.8 %collective-permute-done.2 = f32[32,1024]{1,0:T(8,128)S(1)} collective-permute-done((f32[32,1024]{1,0:T(8,128)S(1)}, f32[32,1024]{1,0:T(8,128)S(1)}, u32[]{:S(2)}, u32[]{:S(2)}) %collective-permute-start.2) | collective-permute-done | bytes 131104 | tf_op jit(solution)/shard_map/ppermute | solution.py:105
  22.8 0.0 copy-start
  22.8 0.0 copy-start.1
  22.8 0.6 %collective-permute-start.3 = (f32[64,1024]{1,0:T(8,128)S(1)}, f32[64,1024]{1,0:T(8,128)S(1)}, u32[]{:S(2)}, u32[]{:S(2)}) collective-permute-start(f32[64,1024]{1,0:T(8,128)S(1)} %pad_maximum_fusion.after_ref.refs_0_), channel_id=1, source_target_pairs={{0,12},{1,13},{2,14},{3,15},{4,8},{5,9},{6,10},{7,11},{8,4},{9,5},... | collective-permute-start | bytes 786440 | tf_op jit(solution)/shard_map/ppermute | solution.py:105
  23.4 2.2 %stage.1.residual_ref = f32[1024,1024]{1,0:T(8,128)S(1)} custom-call(f32[1024,1024]{1,0:T(8,128)} %residual_ref.1, f32[64,1024]{1,0:T(8,128)S(1)} %pad_maximum_fusion.after_ref.refs_0_), custom_call_target="tpu_custom_call" | custom-call | bytes 8388608 | tf_op jit(solution)/shard_map/stage/pallas_call | solution.py:145
  25.6 0.0 collective-permute-done.7.refs_1_
  25.6 0.2 lay.1.v_split
  25.8 5.2 %collective-permute-done.3.refs_1_ = f32[64,1024]{1,0:T(8,128)S(1)} collective-permute-done((f32[64,1024]{1,0:T(8,128)S(1)}, f32[64,1024]{1,0:T(8,128)S(1)}, u32[]{:S(2)}, u32[]{:S(2)}) %collective-permute-start.3) | collective-permute-done | bytes 262176 | tf_op jit(solution)/shard_map/ppermute | solution.py:105
  31.0 0.2 turn.1.t_split
  31.3 0.0 copy-done
  31.3 0.0 copy-done.1
  31.3 2.4 %ladder.1 = f32[1024,1024]{1,0:T(8,128)} custom-call(f32[1024,1024]{1,0:T(8,128)S(1)} %stage.1.residual_ref, bf16[1024,384]{1,0:T(8,128)(2,1)S(1)} %turn.1.t_split, bf16[384,1024]{1,0:T(8,128)(2,1)S(1)} %lay.1.v_split, s32[8,128]{1,0:T(8,128)S(1)} %bitcast.6, s32[8,128]{1,0:T(8,128)S(1)} %bitcast.8), custom_call_target="tpu_custom_call" | custom-call | tf_op jit(solution)/shard_map/ladder/pallas_call | solution.py:175
  (6 shorter events, 0.1 us)
Async XLA Ops:
  1.1 6.5 %collective-permute-start.4 = (f32[8,1024]{1,0:T(8,128)S(1)}, f32[8,1024]{1,0:T(8,128)S(1)}, u32[]{:S(2)}, u32[]{:S(2)}) collective-permute-start(f32[8,1024]{1,0:T(8,128)S(1)} %compact_pair.1), channel_id=1, source_target_pairs={{0,32},{16,48},{32,0},{48,16},{64,96},{80,112},{96,64},{112,80},{1... | collective-permute-start | bytes 98312 | tf_op jit(solution)/shard_map/ppermute | solution.py:106
  4.3 5.3 %collective-permute-start = (f32[8,1024]{1,0:T(8,128)S(1)}, f32[8,1024]{1,0:T(8,128)S(1)}, u32[]{:S(2)}, u32[]{:S(2)}) collective-permute-start(f32[8,1024]{1,0:T(8,128)S(1)} %compact_virt.1), channel_id=1, source_target_pairs={{0,1},{1,0},{2,3},{3,2},{4,5},{5,4},{6,7},{7,6},{8,9},{9,8},{10,11... | collective-permute-start | bytes 98312 | tf_op jit(solution)/shard_map/ppermute | solution.py:105
  7.6 6.9 %collective-permute-start.5 = (f32[16,1024]{1,0:T(8,128)S(1)}, f32[16,1024]{1,0:T(8,128)S(1)}, u32[]{:S(2)}, u32[]{:S(2)}) collective-permute-start(f32[16,1024]{1,0:T(8,128)S(1)} %pad_maximum_fusion.5), channel_id=1, source_target_pairs={{0,64},{16,80},{32,96},{48,112},{64,0},{80,16},{96,32},{112,48},{1... | collective-permute-start | bytes 196616 | tf_op jit(solution)/shard_map/ppermute | solution.py:106
  9.5 8.2 %collective-permute-start.1 = (f32[16,1024]{1,0:T(8,128)S(1)}, f32[16,1024]{1,0:T(8,128)S(1)}, u32[]{:S(2)}, u32[]{:S(2)}) collective-permute-start(f32[16,1024]{1,0:T(8,128)S(1)} %pad_maximum_fusion.4), channel_id=1, source_target_pairs={{0,3},{1,2},{2,1},{3,0},{4,7},{5,6},{6,5},{7,4},{8,11},{9,10},{10,... | collective-permute-start | bytes 196616 | tf_op jit(solution)/shard_map/ppermute | solution.py:105
  14.6 6.3 %collective-permute-start.6 = (f32[32,1024]{1,0:T(8,128)S(1)}, f32[32,1024]{1,0:T(8,128)S(1)}, u32[]{:S(2)}, u32[]{:S(2)}) collective-permute-start(f32[32,1024]{1,0:T(8,128)S(1)} %pad_maximum_fusion.3), channel_id=1, source_target_pairs={{0,192},{16,208},{32,224},{48,240},{64,128},{80,144},{96,160},{112... | collective-permute-start | bytes 393224 | tf_op jit(solution)/shard_map/ppermute | solution.py:106
  17.7 5.1 %collective-permute-start.2 = (f32[32,1024]{1,0:T(8,128)S(1)}, f32[32,1024]{1,0:T(8,128)S(1)}, u32[]{:S(2)}, u32[]{:S(2)}) collective-permute-start(f32[32,1024]{1,0:T(8,128)S(1)} %pad_maximum_fusion.2), channel_id=1, source_target_pairs={{0,4},{1,5},{2,6},{3,7},{4,0},{5,1},{6,2},{7,3},{8,12},{9,13},{10,... | collective-permute-start | bytes 393224 | tf_op jit(solution)/shard_map/ppermute | solution.py:105
  20.9 4.7 %collective-permute-start.7 = (f32[64,1024]{1,0:T(8,128)S(1)}, f32[64,1024]{1,0:T(8,128)S(1)}, u32[]{:S(2)}, u32[]{:S(2)}) collective-permute-start(f32[64,1024]{1,0:T(8,128)S(1)} %pad_maximum_fusion.1.refs_0_), channel_id=1, source_target_pairs={{0,16},{16,0},{32,48},{48,32},{64,80},{80,64},{96,112},{112,96},{1... | collective-permute-start | bytes 786440 | tf_op jit(solution)/shard_map/ppermute | solution.py:106
  22.8 8.5 %copy-start = (s32[1024]{0:T(1024)S(1)}, s32[1024]{0:T(1024)}, u32[]{:S(2)}) copy-start(s32[1024]{0:T(1024)} %param.9) | copy-start | bytes 12292
  22.8 8.5 %copy-start.1 = (s32[1024]{0:T(1024)S(1)}, s32[1024]{0:T(1024)}, u32[]{:S(2)}) copy-start(s32[1024]{0:T(1024)} %param.10) | copy-start | bytes 12292
  22.8 8.2 %collective-permute-start.3 = (f32[64,1024]{1,0:T(8,128)S(1)}, f32[64,1024]{1,0:T(8,128)S(1)}, u32[]{:S(2)}, u32[]{:S(2)}) collective-permute-start(f32[64,1024]{1,0:T(8,128)S(1)} %pad_maximum_fusion.after_ref.refs_0_), channel_id=1, source_target_pairs={{0,12},{1,13},{2,14},{3,15},{4,8},{5,9},{6,10},{7,11},{8,4},{9,5},... | collective-permute-start | bytes 786440 | tf_op jit(solution)/shard_map/ppermute | solution.py:105
